TPU v7x, 256 devices: a whole 4x4x8 slice. The times are simulated.
256 devices in a mesh: dp: 8 (over y, core), expert: 32 (over x, z).
Axes of the slice: x: 4, y: 4, z: 8, core: 2. Of those that a mesh axis runs over, the one named last changes fastest.
Arguments:
- tokens: bfloat16 [32768, 2048], P(('dp', 'expert')), may hold values from -6 to 6
- routes: int32 [32768, 4], P(('dp', 'expert')), may hold values from 0 to 31, all different within a row; in each aligned block of 128 rows (0 to 127, 128 to 255, ...) at most 24 rows name the same one
- combine: float32 [32768, 4], P(('dp', 'expert')), may hold values from 0.2 to 1
- cotangent: bfloat16 [32768, 2048], P(('dp', 'expert')), may hold values from -1.5 to 1.5
- w_gate: bfloat16 [32, 2048, 768], P('expert'), may hold values from -0.125 to 0.125
- w_up: bfloat16 [32, 2048, 768], P('expert'), may hold values from -0.125 to 0.125
- w_down: bfloat16 [32, 768, 2048], P('expert'), may hold values from -0.21875 to 0.21875
Outputs:
- output: bfloat16 [32768, 2048], P(('dp', 'expert'))
- d_tokens: bfloat16 [32768, 2048], P(('dp', 'expert'))
- d_combine: float32 [32768, 4], P(('dp', 'expert'))
- d_w_gate: bfloat16 [32, 2048, 768], P('expert', 'dp')
- d_w_up: bfloat16 [32, 2048, 768], P('expert', 'dp')
- d_w_down: bfloat16 [32, 768, 2048], P('expert', None, 'dp')
Inputs may be any that keep to these rules, and one draw needn't show every extreme that they name: `routes`: each row names 4 different experts. In the rows of one device (aligned blocks of 128 rows) no expert is named by more than 24 rows, a bound that some block reaches.
All inputs are finite; a program needn't handle non-finite values.
Results may differ from a plain program's by a relative error of at most 0.014.
Values may be sent and summed in bfloat16 or wider, within the bound.
A program may use at most 128 MiB of HBM per device.

v0:
```python
import jax
import jax.numpy as jnp
from jax import lax
from jax.sharding import PartitionSpec as P


def slot_map(routes, experts, capacity):
    flat_ids = routes.reshape(-1)
    onehot = (flat_ids[:, None] == jnp.arange(experts, dtype=jnp.int32)[None, :]).astype(jnp.int32)
    before = jnp.cumsum(onehot, axis=0) - onehot
    slots = jnp.sum(before * onehot, axis=1)
    target = flat_ids * capacity + slots
    source = (
        jnp.full((experts * capacity,), -1, jnp.int32)
        .at[target]
        .set(jnp.arange(flat_ids.shape[0], dtype=jnp.int32))
    )
    return (target, source)


def per_device(tokens, routes, combine, cotangent, w_gate, w_up, w_down):
    tok_rows, features = tokens.shape
    per_token = routes.shape[1]
    groups = lax.axis_size("expert")
    local_exp = w_gate.shape[0]
    experts = local_exp * groups
    capacity = 3 * tok_rows * per_token // (2 * experts)
    target, source = slot_map(routes, experts, capacity)
    filled = (source >= 0)[:, None]
    pair_index = jnp.maximum(source, 0)
    owner_row = pair_index // per_token
    outgoing = jnp.where(filled, tokens[owner_row], jnp.zeros((), jnp.bfloat16))
    outgoing = outgoing.reshape(groups, local_exp, capacity, features)
    cot_float = cotangent.astype(jnp.float32)
    scaled = (combine[:, :, None] * cot_float[:, None, :]).reshape(tok_rows * per_token, features)
    outgoing_grad = jnp.where(filled, scaled[pair_index], 0.0).astype(jnp.bfloat16)
    outgoing_grad = outgoing_grad.reshape(groups, local_exp, capacity, features)
    arrived = lax.all_to_all(outgoing, "expert", split_axis=0, concat_axis=0, tiled=True)
    gate_pre = jnp.einsum("secd,edf->secf", arrived, w_gate, preferred_element_type=jnp.float32)
    up_pre = jnp.einsum("secd,edf->secf", arrived, w_up, preferred_element_type=jnp.float32)
    activated = jax.nn.silu(gate_pre)
    hidden = (activated * up_pre).astype(jnp.bfloat16)
    produced = jnp.einsum(
        "secf,efd->secd", hidden, w_down, preferred_element_type=jnp.float32
    ).astype(jnp.bfloat16)
    returned = lax.all_to_all(produced, "expert", split_axis=0, concat_axis=0, tiled=True)
    d_in = lax.all_to_all(outgoing_grad, "expert", split_axis=0, concat_axis=0, tiled=True)
    d_hidden = jnp.einsum("secd,efd->secf", d_in, w_down, preferred_element_type=jnp.float32)
    part_down = jnp.einsum("secf,secd->efd", hidden, d_in, preferred_element_type=jnp.float32)
    sigmoid_g = jax.nn.sigmoid(gate_pre)
    d_gate = (d_hidden * up_pre * sigmoid_g * (1.0 + gate_pre * (1.0 - sigmoid_g))).astype(
        jnp.bfloat16
    )
    d_up = (d_hidden * activated).astype(jnp.bfloat16)
    part_gate = jnp.einsum("secd,secf->edf", arrived, d_gate, preferred_element_type=jnp.float32)
    part_up = jnp.einsum("secd,secf->edf", arrived, d_up, preferred_element_type=jnp.float32)
    d_rows = (
        jnp.einsum("secf,edf->secd", d_gate, w_gate, preferred_element_type=jnp.float32)
        + jnp.einsum("secf,edf->secd", d_up, w_up, preferred_element_type=jnp.float32)
    ).astype(jnp.bfloat16)
    back = lax.all_to_all(d_rows, "expert", split_axis=0, concat_axis=0, tiled=True)
    per_slot = returned.reshape(experts * capacity, features)[target]
    per_slot = per_slot.reshape(tok_rows, per_token, features).astype(jnp.float32)
    output = jnp.sum(combine[:, :, None] * per_slot, axis=1).astype(jnp.bfloat16)
    d_combine = jnp.sum(per_slot * cot_float[:, None, :], axis=2)
    back_slot = back.reshape(experts * capacity, features)[target]
    back_slot = back_slot.reshape(tok_rows, per_token, features).astype(jnp.float32)
    d_tokens = jnp.sum(back_slot, axis=1).astype(jnp.bfloat16)
    sum_gate, sum_up, sum_down = (
        lax.psum_scatter(
            part_gate.astype(jnp.bfloat16), "dp", scatter_dimension=1, tiled=True
        ).astype(jnp.float32),
        lax.psum_scatter(
            part_up.astype(jnp.bfloat16), "dp", scatter_dimension=1, tiled=True
        ).astype(jnp.float32),
        lax.psum_scatter(
            part_down.astype(jnp.bfloat16), "dp", scatter_dimension=2, tiled=True
        ).astype(jnp.float32),
    )
    d_w_down = sum_down.astype(jnp.bfloat16)
    return (
        output,
        d_tokens,
        d_combine,
        sum_gate.astype(jnp.bfloat16),
        sum_up.astype(jnp.bfloat16),
        d_w_down,
    )


def solution(mesh):
    return jax.shard_map(
        per_device,
        mesh=mesh,
        in_specs=(
            P(("dp", "expert"), None),
            P(("dp", "expert"), None),
            P(("dp", "expert"), None),
            P(("dp", "expert"), None),
            P("expert", None, None),
            P("expert", None, None),
            P("expert", None, None),
        ),
        out_specs=(
            P(("dp", "expert"), None),
            P(("dp", "expert"), None),
            P(("dp", "expert"), None),
            P("expert", "dp", None),
            P("expert", "dp", None),
            P("expert", None, "dp"),
        ),
        check_vma=False,
    )
```

profile of v0, /device:TPU:8, one launch (start us, length us, event | category | flops | bytes accessed | tf_op | source)
XLA Modules:
  0.0 427.3 jit_solution(10010816408134451474)
XLA Ops:
  14.2 4.2 mul.87
  18.4 5.3 %mul.88 = f32[512,2048]{1,0:T(8,128)} reshape(f32[128,4,2048]{2,1,0:T(4,128)} %mul.87) | data formatting | bytes 8388608 | tf_op jit(solution)/shard_map/mul | solution.py:35
  27.6 9.0 %gather_fusion.2 = bf16[768,2048]{1,0:T(8,128)(2,1)} fusion(bf16[512,2048]{1,0:T(8,128)(2,1)} %broadcast_multiply_fusion, s32[1024]{0:T(1024)S(1)} %get-tuple-element.21), kind=kCustom, calls=%fused_computation.2 | custom fusion | bytes 6294528 | tf_op jit(solution)/shard_map/gather | solution.py:36
  36.6 8.3 %gather_fusion = bf16[768,2048]{1,0:T(8,128)(2,1)} fusion(bf16[128,2048]{1,0:T(8,128)(2,1)} %param.7, s32[1024]{0:T(1024)S(1)} %get-tuple-element.22), kind=kCustom, calls=%fused_computation | custom fusion | bytes 6294528 | tf_op jit(solution)/shard_map/gather | solution.py:32
  44.9 5.1 %select_convert_fusion = (bf16[32,1,24,2048]{3,2,1,0:T(8,128)(2,1)}, bf16[32,1,24,2048]{3,2,1,0:T(8,128)(2,1)S(1)}) fusion(bf16[32,1,24,2048]{3,2,1,0:T(8,128)(2,1)} %bitcast.177, pred[32,24]{1,0:T(8,128)(4,1)S(1)} %broadcast_in_dim.43, bf16[32,1,24,2048]{3,2,1,0:T(8,128)(2,1)} %bitcast.178), kind=kLoop, calls=%fused_computation.9 | loop fusion | flops 3145728 | bytes 12583680 | tf_op jit(solution)/shard_map/convert_element_type | solution.py:36
  50.0 84.8 %all_to_all.20 = bf16[32,1,24,2048]{3,2,1,0:T(8,128)(2,1)} all-to-all(bf16[32,1,24,2048]{3,2,1,0:T(8,128)(2,1)S(1)} %get-tuple-element.18), channel_id=1, replica_groups=mesh['dp'=8,'expert'=32] {'expert'}, dimensions={0} | all-to-all | bytes 6291456 | tf_op jit(solution)/shard_map/all_to_all | solution.py:38
  134.8 5.2 %all-to-all-start.2 = ((bf16[32,1,24,2048]{3,2,1,0:T(8,128)(2,1)}), bf16[32,1,24,2048]{3,2,1,0:T(8,128)(2,1)}, u32[]{:S(2)}, u32[]{:S(2)}) async-start(bf16[32,1,24,2048]{3,2,1,0:T(8,128)(2,1)} %get-tuple-element.17), calls=%async_computation.2 | async-start | bytes 6291456 | tf_op jit(solution)/shard_map/all_to_all | solution.py:47
  140.0 11.6 %reduce-scatter.4.cloned.1.call-start = ((), (), s32[]{:S(2)}) async-start(), calls=%async_computation.7 | async-start | bytes 3538944 | tf_op jit(solution)/shard_map/reduce_scatter | solution.py:70
  151.6 6.9 %fusion.6 = f32[32,24,768]{2,1,0:T(8,128)} fusion(bf16[1,2048,768]{2,1,0:T(8,128)(2,1)} %param.12, bf16[32,1,24,2048]{3,2,1,0:T(8,128)(2,1)} %all_to_all.20), kind=kOutput, calls=%fused_computation.19 | convolution fusion | flops 2415919104 | bytes 8650752 | tf_op jit(solution)/shard_map/secd,edf->secf/dot_general | solution.py:40
  158.5 55.6 %all-to-all-done.2 = bf16[32,1,24,2048]{3,2,1,0:T(8,128)(2,1)} async-done(((bf16[32,1,24,2048]{3,2,1,0:T(8,128)(2,1)}), bf16[32,1,24,2048]{3,2,1,0:T(8,128)(2,1)}, u32[]{:S(2)}, u32[]{:S(2)}) %all-to-all-start.2) | async-done | bytes 3145760 | tf_op jit(solution)/shard_map/all_to_all | solution.py:47
  214.1 5.6 %fusion.1 = f32[32,24,768]{2,1,0:T(8,128)S(1)} fusion(bf16[32,1,24,2048]{3,2,1,0:T(8,128)(2,1)} %all-to-all-done.2, bf16[1,768,2048]{2,1,0:T(8,128)(2,1)} %param.13), kind=kOutput, calls=%fused_computation.14 | convolution fusion | flops 2415919104 | bytes 8650752 | tf_op jit(solution)/shard_map/secd,efd->secf/dot_general | solution.py:48
  219.8 4.6 %fusion.41 = (bf16[32,24,768]{2,1,0:T(8,128)(2,1)}, bf16[32,1,24,768]{3,2,0,1:T(8,128)(2,1)S(1)}, bf16[32,24,768]{2,1,0:T(8,128)(2,1)}) fusion(f32[32,24,768]{2,1,0:T(8,128)S(1)} %fusion.1, f32[32,24,768]{2,1,0:T(8,128)S(1)} %copy-done.9, bf16[1,2048,768]{2,1,0:T(8,128)(2,1)S(1)} %copy-done, bf16[32,1,24,2048]{3,2,1,0:T(8,128)(2,1)S(1)} %copy-done.2), kind=kOutput, calls=%fused_computation.52 | convolution fusion | flops 2424766464 | bytes 14548992 | tf_op jit(solution)/shard_map/secd,edf->secf/dot_general | solution.py:39
  237.7 5.2 %all-to-all-start.3 = ((bf16[32,1,24,2048]{3,2,1,0:T(8,128)(2,1)}), bf16[32,1,24,2048]{3,2,1,0:T(8,128)(2,1)S(1)}, u32[]{:S(2)}, u32[]{:S(2)}) async-start(bf16[32,1,24,2048]{3,2,1,0:T(8,128)(2,1)} %fusion.19), calls=%async_computation.3 | async-start | bytes 6291456 | tf_op jit(solution)/shard_map/all_to_all | solution.py:61
  242.9 6.7 %fusion.25 = bf16[1,2048,768]{2,1,0:T(8,128)(2,1)} fusion(bf16[32,24,768]{2,1,0:T(8,128)(2,1)} %get-tuple-element.14, bf16[32,1,24,2048]{3,2,1,0:T(8,128)(2,1)} %all_to_all.20), kind=kOutput, calls=%fused_computation.33 | convolution fusion | flops 2417491968 | bytes 7471104 | tf_op jit(solution)/shard_map/secd,secf->edf/dot_general | solution.py:56
  249.7 6.6 %fusion.16 = bf16[32,1,24,2048]{3,2,1,0:T(8,128)(2,1)} fusion(bf16[32,24,768]{2,1,0:T(8,128)(2,1)} %get-tuple-element.16, bf16[1,768,2048]{2,1,0:T(8,128)(2,1)} %param.13), kind=kOutput, calls=%fused_computation.30 | convolution fusion | flops 2417491968 | bytes 7471104 | tf_op jit(solution)/shard_map/secf,efd->secd/dot_general | solution.py:43
  256.3 60.4 %all-to-all-done.3 = bf16[32,1,24,2048]{3,2,1,0:T(8,128)(2,1)S(1)} async-done(((bf16[32,1,24,2048]{3,2,1,0:T(8,128)(2,1)}), bf16[32,1,24,2048]{3,2,1,0:T(8,128)(2,1)S(1)}, u32[]{:S(2)}, u32[]{:S(2)}) %all-to-all-start.3) | async-done | bytes 3145760 | tf_op jit(solution)/shard_map/all_to_all | solution.py:61
  316.6 4.8 %all-to-all-start.1 = ((bf16[32,1,24,2048]{3,2,1,0:T(8,128)(2,1)}), bf16[32,1,24,2048]{3,2,1,0:T(8,128)(2,1)}, u32[]{:S(2)}, u32[]{:S(2)}) async-start(bf16[32,1,24,2048]{3,2,1,0:T(8,128)(2,1)} %fusion.16), calls=%async_computation.1 | async-start | bytes 6291456 | tf_op jit(solution)/shard_map/all_to_all | solution.py:46
  321.7 6.7 %fusion.28 = bf16[1,768,2048]{2,1,0:T(8,128)(2,1)} fusion(bf16[32,24,768]{2,1,0:T(8,128)(2,1)} %get-tuple-element.16, bf16[32,1,24,2048]{3,2,1,0:T(8,128)(2,1)} %all-to-all-done.2), kind=kOutput, calls=%fused_computation.34 | convolution fusion | flops 2417491968 | bytes 7471104 | tf_op jit(solution)/shard_map/secf,secd->efd/dot_general | solution.py:49
  333.9 4.1 reshape.184
  338.0 57.6 %all-to-all-done.1 = bf16[32,1,24,2048]{3,2,1,0:T(8,128)(2,1)} async-done(((bf16[32,1,24,2048]{3,2,1,0:T(8,128)(2,1)}), bf16[32,1,24,2048]{3,2,1,0:T(8,128)(2,1)}, u32[]{:S(2)}, u32[]{:S(2)}) %all-to-all-start.1) | async-done | bytes 3145760 | tf_op jit(solution)/shard_map/all_to_all | solution.py:46
  395.6 7.6 %gather_fusion.1 = bf16[512,2048]{1,0:T(8,128)(2,1)} fusion(bf16[768,2048]{1,0:T(8,128)(2,1)} %bitcast.25, s32[1024]{0:T(1024)S(1)} %pad_clamp_fusion.1), kind=kCustom, calls=%fused_computation.1 | custom fusion | bytes 4196352 | tf_op jit(solution)/shard_map/gather | solution.py:62
  403.2 4.9 %reshape.185 = f32[128,4,2048]{2,1,0:T(4,128)} reshape(bf16[512,2048]{1,0:T(8,128)(2,1)} %gather_fusion.1) | data formatting | bytes 6291456 | tf_op jit(solution)/shard_map/convert_element_type | solution.py:63
  408.1 6.6 %multiply_reduce_fusion = (f32[128,4]{1,0:T(8,128)S(1)}, bf16[128,2048]{1,0:T(8,128)(2,1)}) fusion(f32[128,4,2048]{2,1,0:T(4,128)} %reshape.185, f32[128,2048]{1,0:T(8,128)} %convert_element_type.102, f32[128,4]{1,0:T(8,128)S(1)} %copy-done.4), kind=kLoop, calls=%fused_computation.10 | loop fusion | flops 3931648 | bytes 5771264 | tf_op jit(solution)/shard_map/reduce_sum | solution.py:65
  415.4 5.0 %reduce_sum.44 = bf16[128,2048]{1,0:T(8,128)(2,1)} reduce(bf16[128,4,2048]{2,1,0:T(4,128)(2,1)} %reshape.184, bf16[]{:T(256)} %constant.40.clone.1), dimensions={1}, to_apply=%region_5.6 | reduce | flops 786432 | bytes 2621442 | tf_op jit(solution)/shard_map/reduce_sum | solution.py:68
  (59 shorter events, 30.7 us)
Async XLA Ops:
  7.2 212.6 %copy-start = (bf16[1,2048,768]{2,1,0:T(8,128)(2,1)S(1)}, bf16[1,2048,768]{2,1,0:T(8,128)(2,1)}, u32[]{:S(2)}) copy-start(bf16[1,2048,768]{2,1,0:T(8,128)(2,1)} %param.11) | copy-start | bytes 9437188
  10.8 2.5 copy-start.5
  14.1 9.6 %copy-start.3 = (f32[128,4]{1,0:T(8,128)}, f32[128,4]{1,0:T(8,128)S(1)}, u32[]{:S(2)}) copy-start(f32[128,4]{1,0:T(8,128)S(1)} %copy.32) | copy-start | bytes 6148
  134.8 79.3 %all-to-all-start.2 = ((bf16[32,1,24,2048]{3,2,1,0:T(8,128)(2,1)}), bf16[32,1,24,2048]{3,2,1,0:T(8,128)(2,1)}, u32[]{:S(2)}, u32[]{:S(2)}) async-start(bf16[32,1,24,2048]{3,2,1,0:T(8,128)(2,1)} %get-tuple-element.17), calls=%async_computation.2 | async-start | bytes 6291456 | tf_op jit(solution)/shard_map/all_to_all | solution.py:47
  140.0 280.4 %reduce-scatter.4.cloned.1.call-start = ((), (), s32[]{:S(2)}) async-start(), calls=%async_computation.7 | async-start | bytes 3538944 | tf_op jit(solution)/shard_map/reduce_scatter | solution.py:70
  214.1 5.6 %copy-start.2 = (bf16[32,1,24,2048]{3,2,1,0:T(8,128)(2,1)S(1)}, bf16[32,1,24,2048]{3,2,1,0:T(8,128)(2,1)}, u32[]{:S(2)}) copy-start(bf16[32,1,24,2048]{3,2,1,0:T(8,128)(2,1)} %all_to_all.20) | copy-start | bytes 9437188
  214.1 5.7 %copy-start.9 = (f32[32,24,768]{2,1,0:T(8,128)S(1)}, f32[32,24,768]{2,1,0:T(8,128)}, u32[]{:S(2)}) copy-start(f32[32,24,768]{2,1,0:T(8,128)} %fusion.6) | copy-start | bytes 7077892
  224.3 1.0 copy-start.10
  229.5 4.1 copy-start.7
  229.5 4.1 copy-start.8
  237.7 78.9 %all-to-all-start.3 = ((bf16[32,1,24,2048]{3,2,1,0:T(8,128)(2,1)}), bf16[32,1,24,2048]{3,2,1,0:T(8,128)(2,1)S(1)}, u32[]{:S(2)}, u32[]{:S(2)}) async-start(bf16[32,1,24,2048]{3,2,1,0:T(8,128)(2,1)} %fusion.19), calls=%async_computation.3 | async-start | bytes 6291456 | tf_op jit(solution)/shard_map/all_to_all | solution.py:61
  242.9 177.4 %reduce-scatter.6.cloned.1.call-start = ((), (), s32[]{:S(2)}) async-start(), calls=%async_computation.8 | async-start | bytes 3538944 | tf_op jit(solution)/shard_map/reduce_scatter | solution.py:73
  316.6 79.0 %all-to-all-start.1 = ((bf16[32,1,24,2048]{3,2,1,0:T(8,128)(2,1)}), bf16[32,1,24,2048]{3,2,1,0:T(8,128)(2,1)}, u32[]{:S(2)}, u32[]{:S(2)}) async-start(bf16[32,1,24,2048]{3,2,1,0:T(8,128)(2,1)} %fusion.16), calls=%async_computation.1 | async-start | bytes 6291456 | tf_op jit(solution)/shard_map/all_to_all | solution.py:46
  321.5 98.9 %reduce-scatter.8.cloned.1.call-start = ((), (), s32[]{:S(2)}) async-start(), calls=%async_computation.9 | async-start | bytes 3538944 | tf_op jit(solution)/shard_map/reduce_scatter | solution.py:76
  328.4 2.2 copy-start.6
  403.2 4.9 %copy-start.4 = (f32[128,4]{1,0:T(8,128)S(1)}, f32[128,4]{1,0:T(8,128)}, u32[]{:S(2)}) copy-start(f32[128,4]{1,0:T(8,128)} %copy-done.3) | copy-start | bytes 6148
  403.2 17.2 %copy-start.1 = (bf16[1,2048,768]{2,1,0:T(8,128)(2,1)S(1)}, bf16[1,2048,768]{2,1,0:T(8,128)(2,1)}, u32[]{:S(2)}) copy-start(bf16[1,2048,768]{2,1,0:T(8,128)(2,1)} %param.11) | copy-start | bytes 9437188
Sparse Core Ops, SparseCore 0:
  229.6 31.7 reduce-scatter.3
  264.6 38.1 reduce-scatter.5
  328.5 36.7 reduce-scatter.7
where the time goes:
time: 435 us; the launch traced here: 427 us
  waiting for transfers between devices  174 us (40%)
  blocking collectives  84.8 us (19%)
  local copies, waits for them, and re-layouts  53.4 us (12%)
  matrix products  49.3 us (11%)
  starting transfers between devices  27.1 us (6%)
  other arithmetic  24.7 us (6%)
  between operations  14.3 us (3%)
    all_to_all x1, blocking collectives, per_device(): lax.all_to_all(outgoing, 'expert', split_axis=0, concat_axis=0, tiled=True)  84.8 us
    all_to_all x1, waiting for transfers between devices, per_device(): lax.all_to_all(d_rows, 'expert', split_axis=0, concat_axis=0, tiled=True)  60.4 us
    all_to_all x1, waiting for transfers between devices, per_device(): lax.all_to_all(produced, 'expert', split_axis=0, concat_axis=0, tiled=True)  57.6 us
    all_to_all x1, waiting for transfers between devices, per_device(): lax.all_to_all(outgoing_grad, 'expert', split_axis=0, concat_axis=0, tile...  55.6 us
    reduce_scatter x1, starting transfers between devices, per_device(): lax.psum_scatter(part_gate.astype(jnp.bfloat16), 'dp', scatter_dimension=...  11.6 us
    mul x2, local copies, waits for them, and re-layouts, per_device(): combine[:, :, None] * cot_float[:, None, :]  9.45 us
    gather x1, local copies, waits for them, and re-layouts, per_device(): scaled[pair_index]  8.96 us
  transfers between devices with their start and end apart: 6, of which 3 were waited for; matrix products, arithmetic and copies ran while one was open for 16% of the time, Pallas kernels for 0%

commit v1 on v0

v1 whole, which is shorter than its diff:
```python
import functools

import jax
import jax.numpy as jnp
from jax import lax
from jax.experimental import pallas as pl
from jax.experimental.pallas import tpu as pltpu
from jax.sharding import PartitionSpec as P

MESH = pl.DeviceIdType.MESH
NZ = 8
NX = 4
SUBS = 2
ORDER = [(0, 0), (1, 3), (0, 1), (1, 2), (0, 2), (1, 1), (0, 3), (1, 0)]
BF = jnp.bfloat16
F32 = jnp.float32


def place(m, tokens):
    return m // 2, pl.ds(tokens * (m % 2), tokens)


def neighbours():
    e = lax.axis_index("expert")
    x, z = e // NZ, e % NZ
    zp = x * NZ + (z + 1) % NZ
    zm = x * NZ + (z + NZ - 1) % NZ
    xp = ((x + 1) % NX) * NZ + z
    xm = ((x + NX - 1) % NX) * NZ + z
    return x, z, zp, zm, xp, xm


def greet(devices):
    barrier = pltpu.get_barrier_semaphore()
    for d in devices:
        pl.semaphore_signal(
            barrier, inc=1, device_id={"expert": d}, device_id_type=MESH
        )
    pl.semaphore_wait(barrier, len(devices))


def rcopy(src, dst, send, recv, dev):
    return pltpu.make_async_remote_copy(
        src_ref=src,
        dst_ref=dst,
        send_sem=send,
        recv_sem=recv,
        device_id={"expert": dev},
        device_id_type=MESH,
    )


def row_masks(meta, x, z, cap, blk):
    width = meta.shape[1]
    per = 2 * cap
    col = lax.broadcasted_iota(jnp.int32, (per, width), 1)
    row = lax.broadcasted_iota(jnp.int32, (per, width), 0)
    second = (row >= cap).astype(jnp.int32)
    shift = (col[0:1] >= width // 2).astype(jnp.int32) * 4096
    expert = ((x + blk + 1) % NX) * NZ + z
    ids = row - cap * second + 4096 * second + expert * cap
    return [ids == (meta[k : k + 1, :].astype(jnp.int32) + shift) for k in range(4)]


def dispatch_kernel(
    cap,
    tok_ref,
    cot_ref,
    rc_ref,
    rows_out,
    grad_out,
    picked_out,
    meta_out,
    ag,
    metab,
    smat,
    cmat,
    sx,
    r,
    relay,
    zs,
    zr,
    ms,
    mr,
    xs,
    xr,
    rs,
    rr,
    ls,
):
    tokens, features = tok_ref.shape
    hd = features // 2
    per = 2 * cap
    sub = tokens // SUBS
    x, z, zp, zm, xp, xm = neighbours()
    greet((zp, zm, xp, xm))
    srcs = (tok_ref, cot_ref)
    zdev = (zp, zm)

    def hop(h, s):
        return (s, s + 1) if h == 0 else ((NZ - s) % NZ, NZ - 1 - s)

    def zcopy(st, h, s, u):
        a, b = hop(h, s)
        if s == 0:
            src = srcs[st].at[pl.ds(sub * u, sub), pl.ds(h * hd, hd)]
        else:
            src = ag.at[st, h, a // 2, pl.ds(tokens * (a % 2) + sub * u, sub), :]
        dst = ag.at[st, h, b // 2, pl.ds(tokens * (b % 2) + sub * u, sub), :]
        return rcopy(src, dst, zs.at[st, h, s, u], zr.at[st, h, s, u], zdev[h])

    def mcopy(h, s):
        a, b = hop(h, s)
        (pa, la), (pb, lb) = place(a, tokens), place(b, tokens)
        return rcopy(
            metab.at[pa, :, la], metab.at[pb, :, lb], ms.at[h, s], mr.at[h, s], zdev[h]
        )

    meta_steps = (4, 3)

    def xcopy(st, h, p, i):
        half = pl.ds(h * hd, hd)
        block = (1, 0, 2)[i]
        if i == 0:
            dst = relay.at[st, h, p]
        else:
            dst = r.at[st, p * 4 + i - 1, :, half]
        return rcopy(
            sx.at[st, h, p, pl.ds(block * per, per), :],
            dst,
            xs.at[st, h, p, i],
            xr.at[st, h, p, i],
            (xp if h == 0 else xm, xp, xm)[i],
        )

    def fcopy(st, h, p):
        half = pl.ds(h * hd, hd)
        far = xp if h == 0 else xm
        return rcopy(
            relay.at[st, h, p], r.at[st, p * 4 + 2, :, half], rs.at[st, h, p], rr.at[st, h, p], far
        )

    for h in range(2):
        for u in range(SUBS):
            zcopy(0, h, 0, u).start()

    rc = rc_ref[...]
    experts = NX * NZ
    names = [rc[k : k + 1, :].astype(jnp.int32) for k in range(4)]
    ids = lax.broadcasted_iota(jnp.int32, (experts, tokens), 0)
    hits = [ids == n for n in names]
    count = sum(hit.astype(F32) for hit in hits)
    earlier = lax.broadcasted_iota(jnp.int32, (tokens, tokens), 0)
    later = lax.broadcasted_iota(jnp.int32, (tokens, tokens), 1)
    before = jnp.dot(
        count.astype(BF), (earlier < later).astype(F32).astype(BF), preferred_element_type=F32
    )
    for k in range(4):
        slot = jnp.sum(jnp.where(hits[k], before, 0.0), axis=0, keepdims=True)
        metab[0, k : k + 1, pl.ds(0, tokens)] = rc[k : k + 1, :] * cap + slot
    metab[0, 4:8, pl.ds(0, tokens)] = rc[4:8, :]
    for h in range(2):
        mcopy(h, 0).start()

    for st in range(2):
        for h in range(2):
            ag[st, h, 0, 0:tokens, :] = srcs[st][:, h * hd : (h + 1) * hd]

    ready = set()

    def masks(p):
        if p in ready:
            return
        ready.add(p)
        meta = metab[p]
        for blk in range(NX):
            hit = row_masks(meta, x, z, cap, blk)
            one = functools.reduce(jnp.logical_or, hit)
            weight = sum(jnp.where(hit[k], meta[4 + k : 5 + k, :], 0.0) for k in range(4))
            smat[p, blk * per : (blk + 1) * per, :] = one.astype(F32).astype(BF)
            cmat[p, blk * per : (blk + 1) * per, :] = jnp.broadcast_to(
                jnp.sum(weight, axis=1, keepdims=True), (per, 128)
            )

    def pick(st, h, p):
        masks(p)
        got = jnp.dot(smat[p], ag[st, h, p], preferred_element_type=F32)
        if st == 1:
            got = got * cmat[p, :, 0:1]
        got = got.astype(BF)
        sx[st, h, p] = got
        r[st, p * 4 + 3, :, h * hd : (h + 1) * hd] = got[3 * per :]
        for i in range(3):
            xcopy(st, h, p, i).start()

    def forward(st, h, p):
        xcopy(st, h, p, 0).wait_recv()
        fcopy(st, h, p).start()

    done = {1: [(0, 0)], 2: [(1, 3)], 3: [(0, 1)], 4: [(1, 2)], 5: [(0, 2)], 6: [(1, 1)], 7: [(0, 3), (1, 0)]}
    pending = []
    for st in range(2):
        for d in range(1, NZ):
            if st == 0:
                for h in range(2):
                    if d <= meta_steps[h]:
                        mcopy(h, d - 1).wait_recv()
                        if d < meta_steps[h]:
                            mcopy(h, d).start()
            for u in range(SUBS):
                for h in range(2):
                    zcopy(st, h, d - 1, u).wait_recv()
                    if d < NZ - 1:
                        zcopy(st, h, d, u).start()
                    elif st == 0:
                        zcopy(1, h, 0, u).start()
            for item in pending:
                forward(*item)
            pending = []
            for h, p in done[d]:
                pick(st, h, p)
                pending.append((st, h, p))
    for item in pending:
        forward(*item)

    outs = []
    for st in range(2):
        for h, p in ORDER:
            for i in (1, 2):
                xcopy(st, h, p, i).wait_recv()
            fcopy(st, h, p).wait_recv()
        out = (rows_out, grad_out)[st]
        c = pltpu.make_async_copy(r.at[st], out, ls.at[st])
        c.start()
        outs.append(c)
    for src, dst, i in ((sx.at[1], picked_out, 2), (metab, meta_out, 3)):
        c = pltpu.make_async_copy(src, dst, ls.at[i])
        c.start()
        outs.append(c)
    for st in range(2):
        for h in range(2):
            for s in range(NZ - 1):
                for u in range(SUBS):
                    zcopy(st, h, s, u).wait_send()
        for h, p in ORDER:
            for i in range(3):
                xcopy(st, h, p, i).wait_send()
            fcopy(st, h, p).wait_send()
    for h in range(2):
        for s in range(meta_steps[h]):
            mcopy(h, s).wait_send()
    for c in outs:
        c.wait()


def dispatch(tokens, cotangent, rc, cap):
    n, features = tokens.shape
    hd = features // 2
    per = 2 * cap
    dma = pltpu.SemaphoreType.DMA
    vmem = pl.BlockSpec(memory_space=pltpu.VMEM)
    hbm = pl.BlockSpec(memory_space=pl.ANY)
    return pl.pallas_call(
        functools.partial(dispatch_kernel, cap),
        out_shape=(
            jax.ShapeDtypeStruct((16, per, features), BF),
            jax.ShapeDtypeStruct((16, per, features), BF),
            jax.ShapeDtypeStruct((2, 4, 4 * per, hd), BF),
            jax.ShapeDtypeStruct((4, 8, 2 * n), F32),
        ),
        in_specs=[vmem] * 3,
        out_specs=(hbm,) * 4,
        scratch_shapes=[
            pltpu.VMEM((2, 2, 4, 2 * n, hd), BF),
            pltpu.VMEM((4, 8, 2 * n), F32),
            pltpu.VMEM((4, 4 * per, 2 * n), BF),
            pltpu.VMEM((4, 4 * per, 128), F32),
            pltpu.VMEM((2, 2, 4, 4 * per, hd), BF),
            pltpu.VMEM((2, 16, per, features), BF),
            pltpu.VMEM((2, 2, 4, per, hd), BF),
            dma((2, 2, NZ - 1, SUBS)),
            dma((2, 2, NZ - 1, SUBS)),
            dma((2, 4)),
            dma((2, 4)),
            dma((2, 2, 4, 3)),
            dma((2, 2, 4, 3)),
            dma((2, 2, 4)),
            dma((2, 2, 4)),
            dma((4,)),
        ],
        compiler_params=pltpu.CompilerParams(
            collective_id=0, has_side_effects=True, vmem_limit_bytes=60 * 1024 * 1024
        ),
        name="dispatch",
    )(tokens, cotangent, rc)


def return_kernel(
    cap,
    prod_ref,
    drow_ref,
    picked_ref,
    meta_ref,
    out_ref,
    dtok_ref,
    dcomb_ref,
    q,
    relay,
    part,
    land,
    smat,
    scmat,
    dacc,
    dland,
    zs,
    zr,
    ds_,
    dr,
    xs,
    xr,
    rs,
    rr,
):
    tokens = out_ref.shape[0]
    features = out_ref.shape[1]
    hd = features // 2
    per = 2 * cap
    sub = tokens // SUBS
    x, z, zp, zm, xp, xm = neighbours()
    greet((zp, zm, xp, xm))
    srcs = (prod_ref, drow_ref)
    zdev = (zp, zm)

    def xcopy(st, h, p, i):
        half = pl.ds(h * hd, hd)
        if i == 0:
            dst = relay.at[st, h, p]
        else:
            dst = q.at[st, p, pl.ds((0, 2)[i - 1] * per, per), half]
        return rcopy(
            srcs[st].at[p * 4 + (2, 0, 1)[i], :, half],
            dst,
            xs.at[st, h, p, i],
            xr.at[st, h, p, i],
            (xp if h == 0 else xm, xm, xp)[i],
        )

    def fcopy(st, h, p):
        half = pl.ds(h * hd, hd)
        far = xp if h == 0 else xm
        return rcopy(
            relay.at[st, h, p],
            q.at[st, p, pl.ds(per, per), half],
            rs.at[st, h, p],
            rr.at[st, h, p],
            far,
        )

    def chunk(h, s):
        return s + 1 if h == 0 else NZ - 1 - s

    def zcopy(st, h, s, u):
        m = chunk(h, s)
        src = part.at[st, h, m // 2, pl.ds(tokens * (m % 2) + sub * u, sub), :]
        dst = land.at[st, h, s, pl.ds(sub * u, sub), :]
        return rcopy(src, dst, zs.at[st, h, s, u], zr.at[st, h, s, u], zdev[h])

    def dcopy(s):
        m = s + 1
        pm, lm = place(m, tokens)
        return rcopy(dacc.at[pm, :, lm], dland.at[s], ds_.at[s], dr.at[s], zp)

    for st in range(2):
        for h, p in ORDER:
            for i in range(3):
                xcopy(st, h, p, i).start()

    for p in range(4):
        meta = meta_ref[p]
        for blk in range(NX):
            hit = row_masks(meta, x, z, cap, blk)
            one = functools.reduce(jnp.logical_or, hit)
            weight = sum(jnp.where(hit[k], meta[4 + k : 5 + k, :], 0.0) for k in range(4))
            smat[p, blk * per : (blk + 1) * per, :] = one.astype(F32).astype(BF)
            scmat[p, blk * per : (blk + 1) * per, :] = weight.astype(BF)
        for st in range(2):
            q[st, p, 3 * per :, :] = srcs[st][p * 4 + 3]

    def forward(st, h, p):
        xcopy(st, h, p, 0).wait_recv()
        fcopy(st, h, p).start()

    def scatter(st, h, p):
        for i in (1, 2):
            xcopy(st, h, p, i).wait_recv()
        fcopy(st, h, p).wait_recv()
        mat = scmat if st == 0 else smat
        part[st, h, p] = lax.dot_general(
            mat[p],
            q[st, p, :, h * hd : (h + 1) * hd],
            (((0,), (0,)), ((), ())),
            preferred_element_type=F32,
        ).astype(BF)

    def ring(st, h, s):
        m = chunk(h, s + 1) % NZ
        for u in range(SUBS):
            zcopy(st, h, s, u).wait_recv()
            rows = pl.ds(tokens * (m % 2) + sub * u, sub)
            total = (
                land[st, h, s, pl.ds(sub * u, sub), :].astype(F32)
                + part[st, h, m // 2, rows, :].astype(F32)
            ).astype(BF)
            if s < NZ - 2:
                part[st, h, m // 2, rows, :] = total
                zcopy(st, h, s + 1, u).start()
            else:
                out = (out_ref, dtok_ref)[st]
                out[pl.ds(sub * u, sub), pl.ds(h * hd, hd)] = total

    def weights():
        for p in range(4):
            meta = meta_ref[p]
            for k in range(4):
                dacc[p, k : k + 1, :] = jnp.zeros((1, 2 * tokens), F32)
            dacc[p, 4:8, :] = jnp.zeros((4, 2 * tokens), F32)
            for blk in range(NX):
                rows = pl.ds(blk * per, per)
                v = jnp.zeros((per, 1), F32)
                for h in range(2):
                    a = q[0, p, rows, h * hd : (h + 1) * hd].astype(F32)
                    b = picked_ref[h, p, rows, :].astype(F32)
                    v = v + jnp.sum(a * b, axis=1, keepdims=True)
                hit = row_masks(meta, x, z, cap, blk)
                w = sum(jnp.where(hit[k], meta[4 + k : 5 + k, :], 0.0) for k in range(4))
                c = jnp.sum(w, axis=1, keepdims=True)
                v = v / jnp.where(c > 0.0, c, 1.0)
                for k in range(4):
                    dacc[p, k : k + 1, :] += jnp.sum(
                        jnp.where(hit[k], v, 0.0), axis=0, keepdims=True
                    )

    forward(0, *ORDER[0])
    for st in range(2):
        for i, (h, p) in enumerate(ORDER):
            if i + 1 < len(ORDER):
                forward(st, *ORDER[i + 1])
            elif st == 0:
                forward(1, *ORDER[0])
            scatter(st, h, p)
            if i < 2:
                for u in range(SUBS):
                    zcopy(st, h, 0, u).start()
                if st == 1 and i == 1:
                    for hh in range(2):
                        ring(0, hh, NZ - 2)
                    weights()
                    dcopy(0).start()
            else:
                for hh in range(2):
                    ring(st, hh, i - 2)
                if st == 1:
                    s = i - 2
                    dcopy(s).wait_recv()
                    pm, lm = place(s + 2 if s < NZ - 2 else 0, tokens)
                    dacc[pm, :, lm] += dland[s]
                    dcopy(s + 1).start()
    for hh in range(2):
        ring(1, hh, NZ - 2)
    dcopy(NZ - 2).wait_recv()
    dcomb_ref[...] = dacc[0, :, pl.ds(0, tokens)] + dland[NZ - 2]

    for st in range(2):
        for h in range(2):
            for s in range(NZ - 1):
                for u in range(SUBS):
                    zcopy(st, h, s, u).wait_send()
        for h, p in ORDER:
            for i in range(3):
                xcopy(st, h, p, i).wait_send()
            fcopy(st, h, p).wait_send()
    for s in range(NZ - 1):
        dcopy(s).wait_send()


def give_back(produced, d_rows, picked, meta, tokens, cap):
    features = produced.shape[2]
    hd = features // 2
    per = 2 * cap
    dma = pltpu.SemaphoreType.DMA
    vmem = pl.BlockSpec(memory_space=pltpu.VMEM)
    return pl.pallas_call(
        functools.partial(return_kernel, cap),
        out_shape=(
            jax.ShapeDtypeStruct((tokens, features), BF),
            jax.ShapeDtypeStruct((tokens, features), BF),
            jax.ShapeDtypeStruct((8, tokens), F32),
        ),
        in_specs=[vmem] * 4,
        out_specs=(vmem,) * 3,
        scratch_shapes=[
            pltpu.VMEM((2, 4, 4 * per, features), BF),
            pltpu.VMEM((2, 2, 4, per, hd), BF),
            pltpu.VMEM((2, 2, 4, 2 * tokens, hd), BF),
            pltpu.VMEM((2, 2, NZ - 1, tokens, hd), BF),
            pltpu.VMEM((4, 4 * per, 2 * tokens), BF),
            pltpu.VMEM((4, 4 * per, 2 * tokens), BF),
            pltpu.VMEM((4, 8, 2 * tokens), F32),
            pltpu.VMEM((NZ - 1, 8, tokens), F32),
            dma((2, 2, NZ - 1, SUBS)),
            dma((2, 2, NZ - 1, SUBS)),
            dma((NZ - 1,)),
            dma((NZ - 1,)),
            dma((2, 2, 4, 3)),
            dma((2, 2, 4, 3)),
            dma((2, 2, 4)),
            dma((2, 2, 4)),
        ],
        compiler_params=pltpu.CompilerParams(
            collective_id=1, has_side_effects=True, vmem_limit_bytes=60 * 1024 * 1024
        ),
        name="give_back",
    )(produced, d_rows, picked, meta)


def per_device(tokens, routes, combine, cotangent, w_gate, w_up, w_down):
    n, features = tokens.shape
    per_token = routes.shape[1]
    experts = w_gate.shape[0] * lax.axis_size("expert")
    cap = 3 * n * per_token // (2 * experts)
    rc = jnp.concatenate([routes.T.astype(F32), combine.T], axis=0)
    rows3, grad3, picked, meta = dispatch(tokens, cotangent, rc, cap)
    rows, d_in = rows3.reshape(-1, features), grad3.reshape(-1, features)
    w_gate, w_up, w_down = w_gate[0], w_up[0], w_down[0]
    gate_pre = jnp.dot(rows, w_gate, preferred_element_type=F32)
    up_pre = jnp.dot(rows, w_up, preferred_element_type=F32)
    activated = jax.nn.silu(gate_pre)
    hidden = (activated * up_pre).astype(BF)
    produced = jnp.dot(hidden, w_down, preferred_element_type=F32).astype(BF)
    d_hidden = jnp.dot(d_in, w_down.T, preferred_element_type=F32)
    sig = jax.nn.sigmoid(gate_pre)
    d_gate = (d_hidden * up_pre * sig * (1.0 + gate_pre * (1.0 - sig))).astype(BF)
    d_up = (d_hidden * activated).astype(BF)
    d_rows = (
        jnp.dot(d_gate, w_gate.T, preferred_element_type=F32)
        + jnp.dot(d_up, w_up.T, preferred_element_type=F32)
    ).astype(BF)
    part_down = jnp.dot(hidden.T, d_in, preferred_element_type=F32).astype(BF)
    part_gate = jnp.dot(rows.T, d_gate, preferred_element_type=F32).astype(BF)
    part_up = jnp.dot(rows.T, d_up, preferred_element_type=F32).astype(BF)
    d_w_gate = lax.psum_scatter(part_gate[None], "dp", scatter_dimension=1, tiled=True)
    d_w_up = lax.psum_scatter(part_up[None], "dp", scatter_dimension=1, tiled=True)
    d_w_down = lax.psum_scatter(part_down[None], "dp", scatter_dimension=2, tiled=True)
    output, d_tokens, d_comb = give_back(
        produced.reshape(rows3.shape), d_rows.reshape(rows3.shape), picked, meta, n, cap
    )
    return output, d_tokens, d_comb[:per_token].T, d_w_gate, d_w_up, d_w_down


def solution(mesh):
    row = P(("dp", "expert"), None)
    weight = P("expert", None, None)
    return jax.shard_map(
        per_device,
        mesh=mesh,
        in_specs=(row, row, row, row, weight, weight, weight),
        out_specs=(
            row,
            row,
            row,
            P("expert", "dp", None),
            P("expert", "dp", None),
            P("expert", None, "dp"),
        ),
        check_vma=False,
    )
```

time: 435 us -> 318 us (0.73); the launches traced: 427 us -> 318 us
  Pallas kernels: 0 us -> 253 us
  waiting for transfers between devices: 174 us -> 0.05 us
  blocking collectives: 84.8 us -> 0 us
  local copies, waits for them, and re-layouts: 53.4 us -> 6.05 us
  starting transfers between devices: 27.1 us -> 0.3 us
  other arithmetic: 24.7 us -> 2.19 us
  matrix products: 49.3 us -> 42.3 us
    pallas_call x0 -> x2, Pallas kernels: none -> 253 us  [the longest x1 144 us: give_back(): pl.pallas_call(functools.partial(return_kernel, cap), out_shape=(jax.Shap...]
    all_to_all x3 -> x0, waiting for transfers between devices: 174 us -> none  [the longest x1 60.4 us: per_device(): lax.all_to_all(d_rows, 'expert', split_axis=0, concat_axis=0, tiled=True)]
    all_to_all x1 -> x0, blocking collectives: 84.8 us -> none  [per_device(): lax.all_to_all(outgoing, 'expert', split_axis=0, concat_axis=0, tiled=True)]
    gather x4 -> x0, local copies, waits for them, and re-layouts: 28.2 us -> none  [the longest x1 8.96 us: per_device(): scaled[pair_index]]
    all_to_all x3 -> x0, starting transfers between devices: 15.2 us -> none  [the longest x1 5.19 us: per_device(): lax.all_to_all(outgoing_grad, 'expert', split_axis=0, concat_axis=0, tile...]
    reduce_sum x3 -> x0, other arithmetic: 11.7 us -> none  [the longest x1 6.63 us: per_device(): d_combine = jnp.sum(per_slot * cot_float[:, None, :], axis=2)]
    reduce_scatter x3, starting transfers between devices: 11.9 us -> 0.3 us  [the longest x1 0.22 us: per_device(): lax.psum_scatter(part_gate[None], 'dp', scatter_dimension=1, tiled=True)]
    mul x5 -> x0, local copies, waits for them, and re-layouts: 9.78 us -> none  [the longest x2 9.45 us: per_device(): combine[:, :, None] * cot_float[:, None, :]]
  transfers between devices with their start and end apart: 6 -> 3, of which waited for: 3 -> 0; matrix products, arithmetic and copies ran while one was open for 16% -> 8% of each run, Pallas kernels for 0% -> 45%
where the time goes in v1:
time: 318 us
  Pallas kernels  253 us (80%)
  matrix products  42.3 us (13%)
  between operations  13.9 us (4%)
  local copies, waits for them, and re-layouts  6.05 us (2%)
    pallas_call x1, Pallas kernels, give_back(): pl.pallas_call(functools.partial(return_kernel, cap), out_shape=(jax.Shap...  144 us
    pallas_call x1, Pallas kernels, dispatch(): pl.pallas_call(functools.partial(dispatch_kernel, cap), out_shape=(jax.Sh...  109 us
    dot_general x1, matrix products, per_device(): part_up = jnp.dot(rows.T, d_up, preferred_element_type=F32).astype(BF)  6.61 us
    dot_general x1, matrix products, per_device(): part_gate = jnp.dot(rows.T, d_gate, preferred_element_type=F32).astype(BF)  6.57 us
  transfers between devices with their start and end apart: 3, of which 0 were waited for; matrix products, arithmetic and copies ran while one was open for 8% of the time, Pallas kernels for 45%

profile of v1, /device:TPU:8, one launch (start us, length us, event | category | flops | bytes accessed | tf_op | source)
XLA Modules:
  0.0 317.6 jit_solution(5939022591776983933)
XLA Ops:
  7.2 0.0 copy-start
  7.2 0.0 reduce-scatter.8.cloned.1.call-start
  7.2 0.8 convert_bitcast_fusion
  8.1 1.4 pad_maximum_fusion.rc_ref
  9.4 108.9 %dispatch.1 = (bf16[16,48,2048]{2,1,0:T(8,128)(2,1)}, bf16[16,48,2048]{2,1,0:T(8,128)(2,1)}, bf16[2,4,192,1024]{3,2,1,0:T(8,128)(2,1)}, f32[4,8,256]{2,1,0:T(8,128)}) custom-call(bf16[128,2048]{1,0:T(8,128)(2,1)} %tok_ref.1, bf16[128,2048]{1,0:T(8,128)(2,1)} %cot_ref.1, f32[8,128]{1,0:T(8,128)} %pad_maximum_fusion.rc_ref), custom_call_target="tpu_custom_call" | custom-call | tf_op jit(solution)/shard_map/dispatch/pallas_call | solution.py:263
  118.3 5.6 %fusion.4 = f32[768,768]{1,0:T(8,128)S(1)} fusion(bf16[768,2048]{1,0:T(8,128)(2,1)} %bitcast.47, bf16[1,2048,768]{2,1,0:T(8,128)(2,1)} %param.12), kind=kOutput, calls=%fused_computation.9 | convolution fusion | flops 2415919104 | bytes 8650752 | tf_op jit(solution)/shard_map/dot_general | solution.py:536
  124.0 2.6 fusion.8
  126.6 4.8 %multiply_convert_fusion = (bf16[768,768]{1,0:T(8,128)(2,1)}, bf16[768,768]{1,0:T(8,128)(2,1)}, bf16[768,768]{1,0:T(8,128)(2,1)S(1)}) fusion(f32[768,768]{1,0:T(8,128)S(1)} %fusion.8, f32[768,768]{1,0:T(8,128)S(1)} %fusion.4, bf16[768,2048]{1,0:T(8,128)(2,1)S(1)} %bitcast.51, bf16[1,768,2048]{2,1,0:T(8,128)(2,1)S(1)} %copy-done), kind=kOutput, calls=%fused_computation.18 | convolution fusion | flops 2424766464 | bytes 14548992 | tf_op jit(solution)/shard_map/dot_general | solution.py:540
  131.3 1.0 copy-done.7
  132.3 4.1 %fusion.12 = bf16[1,768,2048]{2,1,0:T(8,128)(2,1)} fusion(bf16[768,768]{1,0:T(8,128)(2,1)S(1)} %get-tuple-element.22, bf16[768,2048]{1,0:T(8,128)(2,1)S(1)} %bitcast.52), kind=kOutput, calls=%fused_computation.17 | convolution fusion | flops 2417491968 | bytes 7471104 | tf_op jit(solution)/shard_map/dot_general | solution.py:548
  136.4 0.0 reduce-scatter.8.cloned.1.call-update
  136.4 0.2 reduce-scatter.4.cloned.1.call-start
  136.7 6.6 %fusion.10 = bf16[1,2048,768]{2,1,0:T(8,128)(2,1)} fusion(bf16[768,2048]{1,0:T(8,128)(2,1)} %bitcast.48, bf16[768,768]{1,0:T(8,128)(2,1)} %get-tuple-element.21), kind=kOutput, calls=%fused_computation.15 | convolution fusion | flops 2417491968 | bytes 7471104 | tf_op jit(solution)/shard_map/dot_general | solution.py:549
  143.2 0.0 reduce-scatter.4.cloned.1.call-update
  143.3 0.0 reduce-scatter.6.cloned.1.call-start
  143.3 6.6 %fusion.11 = bf16[1,2048,768]{2,1,0:T(8,128)(2,1)} fusion(bf16[768,2048]{1,0:T(8,128)(2,1)} %bitcast.49, bf16[768,768]{1,0:T(8,128)(2,1)} %get-tuple-element.20), kind=kOutput, calls=%fused_computation.16 | convolution fusion | flops 2417491968 | bytes 7471104 | tf_op jit(solution)/shard_map/dot_general | solution.py:550
  149.9 0.0 reduce-scatter.6.cloned.1.call-update
  150.0 5.4 %convolution_convert_fusion.3 = bf16[768,2048]{1,0:T(8,128)(2,1)} fusion(bf16[768,768]{1,0:T(8,128)(2,1)} %copy-done.7, bf16[1,768,2048]{2,1,0:T(8,128)(2,1)S(1)} %copy-done), kind=kOutput, calls=%fused_computation.4 | convolution fusion | flops 2417491968 | bytes 7471104 | tf_op jit(solution)/shard_map/dot_general | solution.py:539
  155.4 2.6 fusion.6
  158.1 4.0 %add_convert_fusion = bf16[768,2048]{1,0:T(8,128)(2,1)} fusion(f32[768,2048]{1,0:T(8,128)S(1)} %fusion.6, bf16[768,768]{1,0:T(8,128)(2,1)S(1)} %copy-done.8, bf16[1,2048,768]{2,1,0:T(8,128)(2,1)S(1)} %copy-done.3), kind=kOutput, calls=%fused_computation | convolution fusion | flops 2419064832 | bytes 13762560 | tf_op jit(solution)/shard_map/dot_general | solution.py:546
  162.1 143.9 %give_back.1 = (bf16[128,2048]{1,0:T(8,128)(2,1)}, bf16[128,2048]{1,0:T(8,128)(2,1)}, f32[8,128]{1,0:T(8,128)}) custom-call(bf16[16,48,2048]{2,1,0:T(8,128)(2,1)} %bitcast.44, bf16[16,48,2048]{2,1,0:T(8,128)(2,1)} %bitcast.45, bf16[2,4,192,1024]{3,2,1,0:T(8,128)(2,1)} %get-tuple-element.15.picked_ref, f32[4,8,256]{2,1,0:T(8,128)} %get-tuple-element.16.meta_ref), custom_call_target="tpu_custom_call" | custom-call | tf_op jit(solution)/shard_map/give_back/pallas_call | solution.py:492
  306.0 1.2 slice_bitcast_fusion
  307.3 1.9 copy.15
  309.2 1.9 copy.16
  (19 shorter events, 0.0 us)
Async XLA Ops:
  7.2 119.4 %copy-start = (bf16[1,768,2048]{2,1,0:T(8,128)(2,1)S(1)}, bf16[1,768,2048]{2,1,0:T(8,128)(2,1)}, u32[]{:S(2)}) copy-start(bf16[1,768,2048]{2,1,0:T(8,128)(2,1)} %param.13) | copy-start | bytes 9437188
  7.2 300.1 %reduce-scatter.8.cloned.1.call-start = ((), (), s32[]{:S(2)}) async-start(), calls=%async_computation.5 | async-start | bytes 3538944 | tf_op jit(solution)/shard_map/reduce_scatter | solution.py:553
  118.3 5.6 %copy-start.1 = (bf16[1,2048,768]{2,1,0:T(8,128)(2,1)S(1)}, bf16[1,2048,768]{2,1,0:T(8,128)(2,1)}, u32[]{:S(2)}) copy-start(bf16[1,2048,768]{2,1,0:T(8,128)(2,1)} %param.11) | copy-start | bytes 9437188
  118.3 5.6 %copy-start.4 = (bf16[16,48,2048]{2,1,0:T(8,128)(2,1)S(1)}, bf16[16,48,2048]{2,1,0:T(8,128)(2,1)}, u32[]{:S(2)}) copy-start(bf16[16,48,2048]{2,1,0:T(8,128)(2,1)} %get-tuple-element.13) | copy-start | bytes 9437188
  123.9 2.6 copy-start.5
  131.3 1.0 copy-start.7
  136.4 170.8 %reduce-scatter.4.cloned.1.call-start = ((), (), s32[]{:S(2)}) async-start(), calls=%async_computation.3 | async-start | bytes 3538944 | tf_op jit(solution)/shard_map/reduce_scatter | solution.py:551
  143.3 164.0 %reduce-scatter.6.cloned.1.call-start = ((), (), s32[]{:S(2)}) async-start(), calls=%async_computation.4 | async-start | bytes 3538944 | tf_op jit(solution)/shard_map/reduce_scatter | solution.py:552
  150.0 5.5 %copy-start.2 = (bf16[1,2048,768]{2,1,0:T(8,128)(2,1)S(1)}, bf16[1,2048,768]{2,1,0:T(8,128)(2,1)}, u32[]{:S(2)}) copy-start(bf16[1,2048,768]{2,1,0:T(8,128)(2,1)} %param.11) | copy-start | bytes 9437188
  150.0 5.5 %copy-start.6 = (bf16[768,768]{1,0:T(8,128)(2,1)S(1)}, bf16[768,768]{1,0:T(8,128)(2,1)}, u32[]{:S(2)}) copy-start(bf16[768,768]{1,0:T(8,128)(2,1)} %get-tuple-element.21) | copy-start | bytes 3538948
  155.4 2.7 copy-start.3
  155.4 2.7 copy-start.8
Sparse Core Ops, SparseCore 0:
  136.6 33.4 reduce-scatter.7
  173.2 37.7 reduce-scatter.3
  214.1 37.4 reduce-scatter.5

commit v2 on v1

v2 whole, which is shorter than its diff:
```python
import functools

import jax
import jax.numpy as jnp
from jax import lax
from jax.experimental import pallas as pl
from jax.experimental.pallas import tpu as pltpu
from jax.sharding import PartitionSpec as P

MESH = pl.DeviceIdType.MESH
NZ = 8
NX = 4
SUBS = 4
BF = jnp.bfloat16
F32 = jnp.float32


def neighbours():
    e = lax.axis_index("expert")
    x, z = e // NZ, e % NZ
    zp = x * NZ + (z + 1) % NZ
    zm = x * NZ + (z + NZ - 1) % NZ
    xp = ((x + 1) % NX) * NZ + z
    xm = ((x + NX - 1) % NX) * NZ + z
    return x, z, zp, zm, xp, xm


def greet(devices):
    barrier = pltpu.get_barrier_semaphore()
    for d in devices:
        pl.semaphore_signal(
            barrier, inc=1, device_id={"expert": d}, device_id_type=MESH
        )
    pl.semaphore_wait(barrier, len(devices))


def rcopy(src, dst, send, recv, dev):
    return pltpu.make_async_remote_copy(
        src_ref=src,
        dst_ref=dst,
        send_sem=send,
        recv_sem=recv,
        device_id={"expert": dev},
        device_id_type=MESH,
    )


def row_masks(meta, x, z, cap, blk):
    width = meta.shape[1]
    per = 2 * cap
    col = lax.broadcasted_iota(jnp.int32, (per, width), 1)
    row = lax.broadcasted_iota(jnp.int32, (per, width), 0)
    second = (row >= cap).astype(jnp.int32)
    shift = (col[0:1] >= width // 2).astype(jnp.int32) * 4096
    expert = ((x + blk + 1) % NX) * NZ + z
    ids = row - cap * second + 4096 * second + expert * cap
    return [ids == (meta[k : k + 1, :].astype(jnp.int32) + shift) for k in range(4)]


def dispatch_kernel(
    cap,
    tok_ref,
    cot_ref,
    rc_ref,
    wg_ref,
    wu_ref,
    wd_ref,
    rows_out,
    grad_out,
    picked_out,
    meta_out,
    hid_out,
    dga_out,
    act_out,
    prod_out,
    ag,
    metab,
    smat,
    cmat,
    sx,
    r,
    relay,
    wg,
    wu,
    wd,
    gate,
    hid,
    dga,
    act,
    prod,
    zs,
    zr,
    ms,
    mr,
    xs,
    xr,
    rs,
    rr,
    ls,
    ws,
    os_,
):
    tokens, features = tok_ref.shape
    ff = wg_ref.shape[1]
    hd = features // 2
    per = 2 * cap
    sub = tokens // SUBS
    ft = ff // 3
    nt = features // 4
    x, z, zp, zm, xp, xm = neighbours()
    zdev = (zp, zm)

    loads = []
    for st, src in enumerate((tok_ref, cot_ref)):
        for h in range(2):
            c = pltpu.make_async_copy(
                src.at[:, pl.ds(h * hd, hd)],
                ag.at[st, h, pl.ds(0, tokens), :],
                ls.at[st, h],
            )
            c.start()
            loads.append(c)

    def wload(i, f):
        if i == 2:
            return pltpu.make_async_copy(wd_ref.at[:, pl.ds(f * nt, nt)], wd.at[f], ws.at[i, f])
        src, dst = ((wg_ref, wg), (wu_ref, wu))[i]
        return pltpu.make_async_copy(src.at[:, pl.ds(f * ft, ft)], dst.at[f], ws.at[i, f])

    greet((zp, zm, xp, xm))

    def zcopy(st, h, s, u):
        a = s if h == 0 else (NZ - s) % NZ
        b = s + 1 if h == 0 else NZ - 1 - s
        src = ag.at[st, h, pl.ds(pl.multiple_of(a * tokens + sub * u, sub), sub), :]
        dst = ag.at[st, h, pl.ds(pl.multiple_of(b * tokens + sub * u, sub), sub), :]
        return rcopy(src, dst, zs.at[st, h, s, u], zr.at[st, h, s, u], zdev[h])

    def mcopy(h, s):
        a = s if h == 0 else (NZ - s) % NZ
        b = s + 1 if h == 0 else NZ - 1 - s
        return rcopy(metab.at[a], metab.at[b], ms.at[h, s], mr.at[h, s], zdev[h])

    def xcopy(st, h, p, i):
        far = jnp.where(h == 0, xp, xm)
        dst = relay.at[st, h, p] if i == 0 else r.at[st, h, p * 4 + i - 1]
        return rcopy(
            sx.at[st, h, p, pl.ds((1, 0, 2)[i] * per, per), :],
            dst,
            xs.at[st, h, p, i],
            xr.at[st, h, p, i],
            (far, xp, xm)[i],
        )

    def fcopy(st, h, p):
        far = jnp.where(h == 0, xp, xm)
        return rcopy(relay.at[st, h, p], r.at[st, h, p * 4 + 2], rs.at[st, h, p], rr.at[st, h, p], far)

    for h in range(2):
        loads[h].wait()
        for u in range(SUBS):
            zcopy(0, h, 0, u).start()
    for i, n in ((0, 3), (1, 3), (2, 4)):
        for f in range(n):
            wload(i, f).start()

    rc = rc_ref[...]
    experts = NX * NZ
    names = [rc[k : k + 1, :].astype(jnp.int32) for k in range(4)]
    ids = lax.broadcasted_iota(jnp.int32, (experts, tokens), 0)
    hits = [ids == n for n in names]
    count = sum(hit.astype(F32) for hit in hits)
    earlier = lax.broadcasted_iota(jnp.int32, (tokens, tokens), 0)
    later = lax.broadcasted_iota(jnp.int32, (tokens, tokens), 1)
    before = jnp.dot(
        count.astype(BF), (earlier < later).astype(F32).astype(BF), preferred_element_type=F32
    )
    for k in range(4):
        slot = jnp.sum(jnp.where(hits[k], before, 0.0), axis=0, keepdims=True)
        metab[0, k : k + 1, :] = rc[k : k + 1, :] * cap + slot
    metab[0, 4:8, :] = rc[4:8, :]
    for h in range(2):
        mcopy(h, 0).start()
    for c in loads[2:]:
        c.wait()

    def masks(p):
        meta = jnp.concatenate([metab[2 * p], metab[2 * p + 1]], axis=1)
        for blk in range(NX):
            hit = row_masks(meta, x, z, cap, blk)
            one = functools.reduce(jnp.logical_or, hit)
            weight = sum(jnp.where(hit[k], meta[4 + k : 5 + k, :], 0.0) for k in range(4))
            smat[p, blk * per : (blk + 1) * per, :] = one.astype(F32).astype(BF)
            cmat[p, blk * per : (blk + 1) * per, :] = jnp.broadcast_to(
                jnp.sum(weight, axis=1, keepdims=True), (per, 128)
            )

    def where_at(t):
        st, j = t // 8, t % 8
        h = j % 2
        return st, j, h, jnp.where(h == 0, j // 2, 3 - j // 2)

    def forward(t):
        st, _, h, p = where_at(t)
        xcopy(st, h, p, 0).wait_recv()
        fcopy(st, h, p).start()

    def arrived(st):
        @pl.loop(0, 8)
        def _(i):
            h, p = i // 4, i % 4
            for k in (1, 2):
                xcopy(st, h, p, k).wait_recv()
            fcopy(st, h, p).wait_recv()

    def project(w, f):
        a = jnp.dot(r[0, 0].reshape(-1, hd), w[f, 0:hd], preferred_element_type=F32)
        return a + jnp.dot(r[0, 1].reshape(-1, hd), w[f, hd:], preferred_element_type=F32)

    def gate_tile(f):
        gate[...] = project(wg, f)

    def up_tile(f):
        up = project(wu, f)
        g = gate[...]
        sig = 1.0 / (1.0 + jnp.exp(-g))
        a = g * sig
        act[f] = a.astype(BF)
        hid[f] = (a * up).astype(BF)
        dga[f] = (up * sig * (1.0 + g * (1.0 - sig))).astype(BF)

    def down_tile(h, part):
        n = 2 * h + part
        out = sum(
            jnp.dot(hid[f], wd[n, f * ft : (f + 1) * ft], preferred_element_type=F32)
            for f in range(3)
        )
        prod[h, :, :, part * nt : (part + 1) * nt] = out.astype(BF).reshape(16, per, nt)

    def ring(t, us):
        st, j, _, _ = where_at(t)

        @pl.when(j < NZ - 1)
        def _():
            for u in us:
                for h in range(2):
                    zcopy(st, h, j, u).wait_recv()

                    @pl.when(j < NZ - 2)
                    def _():
                        zcopy(st, h, j + 1, u).start()

                    @pl.when((j == NZ - 2) & (st == 0))
                    def _():
                        zcopy(1, h, 0, u).start()

    @pl.loop(0, 16)
    def _(t):
        st, j, h, p = where_at(t)

        @pl.when(st == 0)
        def _():
            for hh, n in ((0, 4), (1, 3)):

                @pl.when(j < n)
                def _():
                    mcopy(hh, j).wait_recv()

                @pl.when(j + 1 < n)
                def _():
                    mcopy(hh, j + 1).start()

        ring(t, range(0, SUBS // 2))

        @pl.when(t == 10)
        def _():
            arrived(0)
            for i, n in ((0, 3), (1, 3), (2, 4)):
                for f in range(n):
                    wload(i, f).wait()

        tile = (st == 1) & (j >= 2) & (j < 5)
        down = (st == 1) & (j >= 5) & (j < 7)

        @pl.when(tile)
        def _():
            gate_tile(j - 2)

        @pl.when(down)
        def _():
            down_tile(j - 5, 0)

        ring(t, range(SUBS // 2, SUBS))

        @pl.when(t > 0)
        def _():
            forward(t - 1)

        @pl.when(t < 4)
        def _():
            masks(p)

        got = jnp.dot(
            smat[p],
            ag[st, h, pl.ds(pl.multiple_of(p * 2 * tokens, 2 * tokens), 2 * tokens), :],
            preferred_element_type=F32,
        )
        got = (got * jnp.where(st == 1, cmat[p, :, 0:1], 1.0)).astype(BF)
        sx[st, h, p] = got
        r[st, h, p * 4 + 3] = got[3 * per :]
        for i in range(3):
            xcopy(st, h, p, i).start()

        @pl.when(tile)
        def _():
            up_tile(j - 2)

        @pl.when(down)
        def _():
            down_tile(j - 5, 1)

    outs = [(hid, hid_out), (dga, dga_out), (act, act_out), (prod, prod_out), (r.at[0], rows_out), (metab, meta_out), (sx.at[1], picked_out)]
    for i, (src, dst) in enumerate(outs):
        pltpu.make_async_copy(src, dst, os_.at[i]).start()
    forward(15)
    arrived(1)
    last = pltpu.make_async_copy(r.at[1], grad_out, os_.at[len(outs)])
    last.start()

    @pl.loop(0, 2)
    def _(st):
        for h in range(2):

            @pl.loop(0, NZ - 1)
            def _(s):
                for u in range(SUBS):
                    zcopy(st, h, s, u).wait_send()

        @pl.loop(0, 8)
        def _(i):
            for k in range(3):
                xcopy(st, i // 4, i % 4, k).wait_send()
            fcopy(st, i // 4, i % 4).wait_send()

    for h, n in ((0, 4), (1, 3)):
        for s in range(n):
            mcopy(h, s).wait_send()
    for i, (src, dst) in enumerate(outs):
        pltpu.make_async_copy(src, dst, os_.at[i]).wait()
    last.wait()


def dispatch(tokens, cotangent, rc, w_gate, w_up, w_down, cap):
    n, features = tokens.shape
    ff = w_gate.shape[1]
    hd = features // 2
    per = 2 * cap
    rows = 16 * per
    ft, nt = ff // 3, features // 4
    dma = pltpu.SemaphoreType.DMA
    vmem = pl.BlockSpec(memory_space=pltpu.VMEM)
    hbm = pl.BlockSpec(memory_space=pl.ANY)
    halves = jax.ShapeDtypeStruct((2, 16, per, hd), BF)
    hidden = jax.ShapeDtypeStruct((3, rows, ft), BF)
    return pl.pallas_call(
        functools.partial(dispatch_kernel, cap),
        out_shape=(
            halves,
            halves,
            jax.ShapeDtypeStruct((2, 4, 4 * per, hd), BF),
            jax.ShapeDtypeStruct((NZ, 8, n), F32),
            hidden,
            hidden,
            hidden,
            halves,
        ),
        in_specs=[hbm, hbm, vmem, hbm, hbm, hbm],
        out_specs=(hbm,) * 8,
        scratch_shapes=[
            pltpu.VMEM((2, 2, NZ * n, hd), BF),
            pltpu.VMEM((NZ, 8, n), F32),
            pltpu.VMEM((4, 4 * per, 2 * n), BF),
            pltpu.VMEM((4, 4 * per, 128), F32),
            pltpu.VMEM((2, 2, 4, 4 * per, hd), BF),
            pltpu.VMEM((2, 2, 16, per, hd), BF),
            pltpu.VMEM((2, 2, 4, per, hd), BF),
            pltpu.VMEM((3, features, ft), BF),
            pltpu.VMEM((3, features, ft), BF),
            pltpu.VMEM((4, ff, nt), BF),
            pltpu.VMEM((rows, ft), F32),
            pltpu.VMEM((3, rows, ft), BF),
            pltpu.VMEM((3, rows, ft), BF),
            pltpu.VMEM((3, rows, ft), BF),
            pltpu.VMEM((2, 16, per, hd), BF),
            dma((2, 2, NZ - 1, SUBS)),
            dma((2, 2, NZ - 1, SUBS)),
            dma((2, 4)),
            dma((2, 4)),
            dma((2, 2, 4, 3)),
            dma((2, 2, 4, 3)),
            dma((2, 2, 4)),
            dma((2, 2, 4)),
            dma((2, 2)),
            dma((3, 4)),
            dma((8,)),
        ],
        compiler_params=pltpu.CompilerParams(
            collective_id=0, has_side_effects=True, vmem_limit_bytes=62 * 1024 * 1024
        ),
        name="dispatch",
    )(tokens, cotangent, rc, w_gate, w_up, w_down)


def return_kernel(
    cap,
    prod_ref,
    drow_ref,
    picked_ref,
    meta_ref,
    out_ref,
    dtok_ref,
    dcomb_ref,
    q,
    relay,
    part,
    land,
    smat,
    stmat,
    dacc,
    dland,
    zs,
    zr,
    ds_,
    dr,
    xs,
    xr,
    rs,
    rr,
    ls,
):
    tokens, features = out_ref.shape
    hd = features // 2
    per = 2 * cap
    sub = tokens // SUBS
    x, z, zp, zm, xp, xm = neighbours()
    zdev = (zp, zm)
    srcs = (prod_ref, drow_ref)
    greet((zp, zm, xp, xm))

    def where_at(t):
        st, j = t // 8, t % 8
        h = j % 2
        return st, j, h, jnp.where(h == 0, j // 2, 3 - j // 2)

    def xcopy(st, h, p, i, src):
        far = jnp.where(h == 0, xp, xm)
        dst = relay.at[st, h, p] if i == 0 else q.at[st, h, p, pl.ds((0, 2)[i - 1] * per, per), :]
        return rcopy(
            src.at[h, p * 4 + (2, 0, 1)[i]],
            dst,
            xs.at[st, h, p, i],
            xr.at[st, h, p, i],
            (far, xm, xp)[i],
        )

    def fcopy(st, h, p):
        far = jnp.where(h == 0, xp, xm)
        return rcopy(
            relay.at[st, h, p],
            q.at[st, h, p, pl.ds(per, per), :],
            rs.at[st, h, p],
            rr.at[st, h, p],
            far,
        )

    def own(st, h, p, src):
        return pltpu.make_async_copy(
            src.at[h, p * 4 + 3], q.at[st, h, p, pl.ds(3 * per, per), :], ls.at[st, h, p]
        )

    def send(t):
        st, _, h, p = where_at(t)
        for i in range(2):

            @pl.when(st == i)
            def _():
                for k in range(3):
                    xcopy(i, h, p, k, srcs[i]).start()
                own(i, h, p, srcs[i]).start()

    def forward(t):
        st, _, h, p = where_at(t)
        xcopy(st, h, p, 0, prod_ref).wait_recv()
        fcopy(st, h, p).start()

    def chunk(h, s):
        return s + 1 if h == 0 else NZ - 1 - s

    def zcopy(st, h, s, u):
        m = chunk(h, s)
        src = part.at[st, h, pl.ds(pl.multiple_of(m * tokens + sub * u, sub), sub), :]
        dst = land.at[st, h, s, pl.ds(sub * u, sub), :]
        return rcopy(src, dst, zs.at[st, h, s, u], zr.at[st, h, s, u], zdev[h])

    def dcopy(s):
        return rcopy(dacc.at[s + 1], dland.at[s], ds_.at[s], dr.at[s], zp)

    def meta_of(p):
        return jnp.concatenate([meta_ref[2 * p], meta_ref[2 * p + 1]], axis=1)

    def mats(p):
        meta = meta_of(p)
        for blk in range(NX):
            hit = row_masks(meta, x, z, cap, blk)
            one = functools.reduce(jnp.logical_or, hit)
            weight = sum(jnp.where(hit[k], meta[4 + k : 5 + k, :], 0.0) for k in range(4))
            smat[0, blk * per : (blk + 1) * per, :] = weight
            smat[1, blk * per : (blk + 1) * per, :] = one.astype(F32)
        for i in range(2):
            stmat[i, p] = smat[i].T.astype(BF)

    def scatter(t):
        st, _, h, p = where_at(t)
        for k in (1, 2):
            xcopy(st, h, p, k, prod_ref).wait_recv()
        fcopy(st, h, p).wait_recv()
        own(st, h, p, prod_ref).wait()
        rows = pl.ds(pl.multiple_of(p * 2 * tokens, 2 * tokens), 2 * tokens)
        part[st, h, rows, :] = jnp.dot(
            stmat[st, p], q[st, h, p], preferred_element_type=F32
        ).astype(BF)

    def ring(st, s, us):
        for u in us:
            for h in range(2):
                m = chunk(h, s + 1)
                rows = pl.ds(pl.multiple_of(m * tokens + sub * u, sub), sub)
                zcopy(st, h, s, u).wait_recv()
                part[st, h, rows, :] += land[st, h, s, pl.ds(sub * u, sub), :]
                zcopy(st, h, s + 1, u).start()

    def finish(st, us):
        out = (out_ref, dtok_ref)[st]
        for u in us:
            rows = pl.ds(sub * u, sub)
            for h in range(2):
                zcopy(st, h, NZ - 2, u).wait_recv()
                out[rows, h * hd : (h + 1) * hd] = part[st, h, rows, :] + land[st, h, NZ - 2, rows, :]

    def weights(p):
        meta = meta_of(p)
        total = [jnp.zeros((1, 2 * tokens), F32)] * 4
        for blk in range(NX):
            v = jnp.zeros((per, 1), F32)
            for h in range(2):
                a = q[0, h, p, blk * per : (blk + 1) * per, :].astype(F32)
                b = picked_ref[h, p, blk * per : (blk + 1) * per, :].astype(F32)
                v = v + jnp.sum(a * b, axis=1, keepdims=True)
            hit = row_masks(meta, x, z, cap, blk)
            w = sum(jnp.where(hit[k], meta[4 + k : 5 + k, :], 0.0) for k in range(4))
            c = jnp.sum(w, axis=1, keepdims=True)
            v = v / jnp.where(c > 0.0, c, 1.0)
            for k in range(4):
                total[k] = total[k] + jnp.sum(jnp.where(hit[k], v, 0.0), axis=0, keepdims=True)
        for k in range(4):
            for i in range(2):
                dacc[2 * p + i, k : k + 1, :] = total[k][:, i * tokens : (i + 1) * tokens]
        for i in range(2):
            dacc[2 * p + i, 4:8, :] = jnp.zeros((4, tokens), F32)

    send(0)
    send(1)
    mats(0)
    forward(0)
    send(2)

    @pl.loop(1, 4)
    def _(p):
        mats(p)

    forward(1)

    @pl.loop(0, 16)
    def _(t):
        st, j, h, p = where_at(t)

        @pl.when(t + 3 < 16)
        def _():
            send(t + 3)

        scatter(t)

        @pl.when(j >= 2)
        def _():
            ring(st, j - 2, range(0, SUBS // 2))

        @pl.when(t + 2 < 16)
        def _():
            forward(t + 2)

        @pl.when(j >= 2)
        def _():
            ring(st, j - 2, range(SUBS // 2, SUBS))

        @pl.when(j < 2)
        def _():
            for u in range(SUBS):
                for hh in range(2):

                    @pl.when(h == hh)
                    def _():
                        zcopy(st, hh, 0, u).start()

        @pl.when(t == 9)
        def _():
            finish(0, range(SUBS))

        @pl.when(t == 9)
        def _():
            @pl.loop(0, 4)
            def _(i):
                weights(i)

            dcopy(0).start()

        @pl.when(t >= 10)
        def _():
            s = t - 10
            dcopy(s).wait_recv()
            dacc[s + 2] += dland[s]
            dcopy(s + 1).start()

    finish(1, range(SUBS))
    dcopy(NZ - 2).wait_recv()
    dcomb_ref[...] = dacc[0] + dland[NZ - 2]

    @pl.loop(0, 2)
    def _(st):
        for h in range(2):

            @pl.loop(0, NZ - 1)
            def _(s):
                for u in range(SUBS):
                    zcopy(st, h, s, u).wait_send()

        @pl.loop(0, 8)
        def _(i):
            for k in range(3):
                xcopy(st, i // 4, i % 4, k, prod_ref).wait_send()
            fcopy(st, i // 4, i % 4).wait_send()

    @pl.loop(0, NZ - 1)
    def _(s):
        dcopy(s).wait_send()


def give_back(produced, d_rows, picked, meta, tokens, cap):
    features = 2 * produced.shape[3]
    hd = features // 2
    per = 2 * cap
    dma = pltpu.SemaphoreType.DMA
    vmem = pl.BlockSpec(memory_space=pltpu.VMEM)
    hbm = pl.BlockSpec(memory_space=pl.ANY)
    return pl.pallas_call(
        functools.partial(return_kernel, cap),
        out_shape=(
            jax.ShapeDtypeStruct((tokens, features), BF),
            jax.ShapeDtypeStruct((tokens, features), BF),
            jax.ShapeDtypeStruct((8, tokens), F32),
        ),
        in_specs=[hbm, hbm, vmem, vmem],
        out_specs=(vmem,) * 3,
        scratch_shapes=[
            pltpu.VMEM((2, 2, 4, 4 * per, hd), BF),
            pltpu.VMEM((2, 2, 4, per, hd), BF),
            pltpu.VMEM((2, 2, NZ * tokens, hd), BF),
            pltpu.VMEM((2, 2, NZ - 1, tokens, hd), BF),
            pltpu.VMEM((2, 4 * per, 2 * tokens), F32),
            pltpu.VMEM((2, 4, 2 * tokens, 4 * per), BF),
            pltpu.VMEM((NZ, 8, tokens), F32),
            pltpu.VMEM((NZ - 1, 8, tokens), F32),
            dma((2, 2, NZ - 1, SUBS)),
            dma((2, 2, NZ - 1, SUBS)),
            dma((NZ - 1,)),
            dma((NZ - 1,)),
            dma((2, 2, 4, 3)),
            dma((2, 2, 4, 3)),
            dma((2, 2, 4)),
            dma((2, 2, 4)),
            dma((2, 2, 4)),
        ],
        compiler_params=pltpu.CompilerParams(
            collective_id=1, has_side_effects=True, vmem_limit_bytes=62 * 1024 * 1024
        ),
        name="give_back",
    )(produced, d_rows, picked, meta)


def per_device(tokens, routes, combine, cotangent, w_gate, w_up, w_down):
    n, features = tokens.shape
    per_token = routes.shape[1]
    experts = w_gate.shape[0] * lax.axis_size("expert")
    cap = 3 * n * per_token // (2 * experts)
    per = 2 * cap
    rc = jnp.concatenate([routes.T.astype(F32), combine.T], axis=0)
    w_gate, w_up, w_down = w_gate[0], w_up[0], w_down[0]
    rows2, grad2, picked, meta, hid3, dga3, act3, produced = dispatch(
        tokens, cotangent, rc, w_gate, w_up, w_down, cap
    )

    def whole(a):
        return jnp.concatenate([a[0], a[1]], axis=-1).reshape(16 * per, features)

    def wide(a):
        return jnp.concatenate([a[0], a[1], a[2]], axis=-1)

    rows, d_in = whole(rows2), whole(grad2)
    hidden = wide(hid3)
    d_hidden = jnp.dot(d_in, w_down.T, preferred_element_type=F32)
    d_gate = (d_hidden * wide(dga3).astype(F32)).astype(BF)
    d_up = (d_hidden * wide(act3).astype(F32)).astype(BF)
    d_rows = (
        jnp.dot(d_gate, w_gate.T, preferred_element_type=F32)
        + jnp.dot(d_up, w_up.T, preferred_element_type=F32)
    ).astype(BF)
    d_rows = jnp.stack([d_rows[:, : features // 2], d_rows[:, features // 2 :]]).reshape(produced.shape)
    part_down = jnp.dot(hidden.T, d_in, preferred_element_type=F32).astype(BF)
    part_gate = jnp.dot(rows.T, d_gate, preferred_element_type=F32).astype(BF)
    part_up = jnp.dot(rows.T, d_up, preferred_element_type=F32).astype(BF)
    d_w_gate = lax.psum_scatter(part_gate[None], "dp", scatter_dimension=1, tiled=True)
    d_w_up = lax.psum_scatter(part_up[None], "dp", scatter_dimension=1, tiled=True)
    d_w_down = lax.psum_scatter(part_down[None], "dp", scatter_dimension=2, tiled=True)
    output, d_tokens, d_comb = give_back(produced, d_rows, picked, meta, n, cap)
    return output, d_tokens, d_comb[:per_token].T, d_w_gate, d_w_up, d_w_down


def solution(mesh):
    row = P(("dp", "expert"), None)
    weight = P("expert", None, None)
    return jax.shard_map(
        per_device,
        mesh=mesh,
        in_specs=(row, row, row, row, weight, weight, weight),
        out_specs=(
            row,
            row,
            row,
            P("expert", "dp", None),
            P("expert", "dp", None),
            P("expert", None, "dp"),
        ),
        check_vma=False,
    )
```

time: 318 us -> 278 us (0.87)
  Pallas kernels: 253 us -> 211 us
  matrix products: 42.3 us -> 26.7 us
  local copies, waits for them, and re-layouts: 6.05 us -> 21.5 us
    pallas_call x1, Pallas kernels: 144 us -> 101 us  [give_back(): pl.pallas_call(functools.partial(return_kernel, cap), out_shape=(jax.Shap...]
    dot_general x3 -> x0, matrix products: 13.6 us -> none  [the longest x1 5.58 us: per_device(): up_pre = jnp.dot(rows, w_up, preferred_element_type=F32)]
    unnamed x20 -> x38, local copies, waits for them, and re-layouts: 4.8 us -> 11.4 us
    slice x0 -> x2, local copies, waits for them, and re-layouts: none -> 4.68 us  [the longest x1 4.31 us: whole(): return jnp.concatenate([a[0], a[1]], axis=-1).reshape(16 * per, features)]
    squeeze x0 -> x2, local copies, waits for them, and re-layouts: none -> 4.22 us  [wide(): return jnp.concatenate([a[0], a[1], a[2]], axis=-1)]
  transfers between devices with their start and end apart: 3 -> 3, of which waited for: 0 -> 0; matrix products, arithmetic and copies ran while one was open for 8% -> 10% of each run, Pallas kernels for 45% -> 37%
where the time goes in v2:
time: 278 us; the launch traced here: 277 us
  Pallas kernels  211 us (76%)
  matrix products  26.7 us (10%)
  local copies, waits for them, and re-layouts  21.5 us (8%)
  between operations  13.9 us (5%)
  other arithmetic  3.89 us (1%)
    pallas_call x1, Pallas kernels, dispatch(): pl.pallas_call(functools.partial(dispatch_kernel, cap), out_shape=(halves...  110 us
    pallas_call x1, Pallas kernels, give_back(): pl.pallas_call(functools.partial(return_kernel, cap), out_shape=(jax.Shap...  101 us
    unnamed x38, local copies, waits for them, and re-layouts  11.4 us
    dot_general x1, matrix products, per_device(): part_up = jnp.dot(rows.T, d_up, preferred_element_type=F32).astype(BF)  6.19 us
  transfers between devices with their start and end apart: 3, of which 0 were waited for; matrix products, arithmetic and copies ran while one was open for 10% of the time, Pallas kernels for 37%

profile of v2, /device:TPU:8, one launch (start us, length us, event | category | flops | bytes accessed | tf_op | source)
XLA Modules:
  0.0 277.5 jit_solution(16329193071745303522)
XLA Ops:
  7.2 0.7 convert_bitcast_fusion
  7.9 1.3 pad_maximum_fusion.7.rc_ref
  9.2 109.6 %dispatch.1 = (bf16[2,16,48,1024]{3,2,1,0:T(8,128)(2,1)}, bf16[2,16,48,1024]{3,2,1,0:T(8,128)(2,1)}, bf16[2,4,192,1024]{3,2,1,0:T(8,128)(2,1)}, f32[8,8,128]{2,1...) custom-call(bf16[128,2048]{1,0:T(8,128)(2,1)} %tok_ref.1, ...), custom_call_target="tpu_custom_call" | custom-call | tf_op jit(solution)/shard_map/dispatch/pallas_call | solution.py:365
  118.8 2.8 slice_bitcast_fusion.2
  121.6 4.3 %fusion.17 = (bf16[1,16,48,1024]{3,2,1,0:T(8,128)(2,1)}, bf16[1,16,48,1024]{3,2,1,0:T(8,128)(2,1)}, bf16[1,16,48,1024]{3,2,1,0:T(8,128)(2,1)S(1)}, bf16[1,16,48,1024]{3,2,1,0:T(8,128)(2,1)S(1)}) fusion(bf16[2,16,48,1024]{3,2,1,0:T(8,128)(2,1)S(1)} %copy-done.3, bf16[2,16,48,1024]{3,2,1,0:T(8,128)(2,1)} %get-tuple-element.18), kind=kLoop, calls=%fused_computation.38 | loop fusion | bytes 12582912 | tf_op jit(solution)/shard_map/slice | solution.py:712
  125.9 1.2 copy-done.8
  127.5 4.2 %fusion.2 = bf16[1,768,2048]{2,1,0:T(8,128)(2,1)} fusion(bf16[768,1024]{1,0:T(8,128)(2,1)S(1)} %bitcast.53, bf16[768,1024]{1,0:T(8,128)(2,1)S(1)} %bitcast.55, bf16[768,256]{1,0:T(8,128)(2,1)S(1)} %get-tuple-element.35, bf16[768,256]{1,0:T(8,128)(2,1)S(1)} %get-tuple-element.36, bf16[768,256]{1,0:T(8,128)(2,1)S(1)} %get-tuple-element.34), kind=kOutput, calls=%fused_computation.9 | convolution fusion | flops 2427322368 | bytes 7471104 | tf_op jit(solution)/shard_map/dot_general | solution.py:727
  131.9 1.5 slice_bitcast_fusion.8
  133.4 0.5 copy-done
  133.9 0.5 copy-done.9
  134.5 4.5 %fusion.3 = f32[768,768]{1,0:T(8,128)S(1)} fusion(bf16[768,1024]{1,0:T(8,128)(2,1)S(1)} %bitcast.54, bf16[768,1024]{1,0:T(8,128)(2,1)} %bitcast.56, bf16[1,768,2048]{2,1,0:T(8,128)(2,1)S(1)} %copy-done), kind=kOutput, calls=%fused_computation.12 | convolution fusion | flops 2422210560 | bytes 8650752 | tf_op jit(solution)/shard_map/dot_general | solution.py:719
  139.0 1.4 copy-done.16
  140.4 4.5 %fusion = bf16[1,2048,768]{2,1,0:T(8,128)(2,1)} fusion(bf16[768,1024]{1,0:T(8,128)(2,1)S(1)} %bitcast.51, bf16[768,1024]{1,0:T(8,128)(2,1)S(1)} %bitcast.49, f32[768,768]{1,0:T(8,128)S(1)} %fusion.3, bf16[768,256]{1,0:T(8,128)(2,1)S(1)} %get-tuple-element.41, bf16[768,256]{1,0:T(8,128)(2,1)S(1)} %get-tuple-element.42, bf16[768,256]{1,0:T(8,128)(2,1)S(1)} %get-tuple-element.40), kind=kOutput, calls=%fused_computation.7 | convolution fusion | flops 2428502016 | bytes 9830400 | tf_op jit(solution)/shard_map/dot_general | solution.py:728
  145.2 1.1 copy-done.5
  146.3 0.5 copy-done.7
  146.8 6.2 %fusion.1 = bf16[1,2048,768]{2,1,0:T(8,128)(2,1)} fusion(bf16[768,1024]{1,0:T(8,128)(2,1)S(1)} %bitcast.52, bf16[768,1024]{1,0:T(8,128)(2,1)S(1)} %bitcast.50, f32[768,768]{1,0:T(8,128)} %copy-done.16, bf16[768,256]{1,0:T(8,128)(2,1)} %get-tuple-element.44, bf16[768,256]{1,0:T(8,128)(2,1)S(1)} %get-tuple-element.43, bf16[768,256]{1,0:T(8,128)(2,1)} %get-tuple-element.45), kind=kOutput, calls=%fused_computation.8 | convolution fusion | flops 2428502016 | bytes 9830400 | tf_op jit(solution)/shard_map/dot_general | solution.py:729
  153.0 1.9 copy-done.1
  154.9 4.5 %fusion.15 = f32[768,2048]{1,0:T(8,128)S(1)} fusion(bf16[1,2048,768]{2,1,0:T(8,128)(2,1)S(1)} %copy-done.1, f32[768,768]{1,0:T(8,128)} %copy-done.16, bf16[768,256]{1,0:T(8,128)(2,1)} %copy-done.14, bf16[768,256]{1,0:T(8,128)(2,1)} %copy-done.15, bf16[768,256]{1,0:T(8,128)(2,1)} %copy-done.13), kind=kOutput, calls=%fused_computation.36 | convolution fusion | flops 2420637696 | bytes 12976128 | tf_op jit(solution)/shard_map/dot_general | solution.py:723
  159.4 2.9 %add_convert_fusion = bf16[768,2048]{1,0:T(8,128)(2,1)S(1)} fusion(f32[768,2048]{1,0:T(8,128)S(1)} %fusion.15, bf16[1,2048,768]{2,1,0:T(8,128)(2,1)S(1)} %copy-done.2, f32[768,768]{1,0:T(8,128)S(1)} %copy-done.17, bf16[768,256]{1,0:T(8,128)(2,1)S(1)} %copy-done.11, bf16[768,256]{1,0:T(8,128)(2,1)S(1)} %get-tuple-element.43, bf16[768,256]{1,0:T(8,128)(2,1)S(1)} %copy-done.12), kind=kOutput, calls=%fused_computation | convolution fusion | flops 2423783424 | bytes 16121856 | tf_op jit(solution)/shard_map/dot_general | solution.py:724
  162.7 1.9 pad_maximum_fusion.1.drow_ref
  164.6 101.3 %give_back.1 = (bf16[128,2048]{1,0:T(8,128)(2,1)}, bf16[128,2048]{1,0:T(8,128)(2,1)}, f32[8,128]{1,0:T(8,128)}) custom-call(bf16[2,16,48,1024]{3,2,1,0:T(8,128)(2,1)} %get-tuple-element.17.prod_ref, bf16[2,16,48,1024]{3,2,1,0:T(8,128)(2,1)} %pad_maximum_fusion.1.drow_ref, bf16[2,4,192,1024]{3,2,1,0:T(8,128)(2,1)} %get-tuple-element.21.picked_ref, ...), custom_call_target="tpu_custom_call" | custom-call | tf_op jit(solution)/shard_map/give_back/pallas_call | solution.py:664
  265.9 1.3 slice_bitcast_fusion.9
  267.2 1.9 copy.15
  269.1 1.9 copy.16
  (39 shorter events, 1.4 us)
Async XLA Ops:
  7.2 260.0 %reduce-scatter.8.cloned.1.call-start = ((), (), s32[]{:S(2)}) async-start(), calls=%async_computation.5 | async-start | bytes 3538944 | tf_op jit(solution)/shard_map/reduce_scatter | solution.py:732
  118.8 2.8 %copy-start.3 = (bf16[2,16,48,1024]{3,2,1,0:T(8,128)(2,1)S(1)}, bf16[2,16,48,1024]{3,2,1,0:T(8,128)(2,1)}, u32[]{:S(2)}) copy-start(bf16[2,16,48,1024]{3,2,1,0:T(8,128)(2,1)} %get-tuple-element.26) | copy-start | bytes 9437188
  125.9 1.2 copy-start.8
  125.9 1.6 copy-start.10
  131.7 2.2 copy-start
  131.7 135.5 %reduce-scatter.4.cloned.1.call-start = ((), (), s32[]{:S(2)}) async-start(), calls=%async_computation.3 | async-start | bytes 3538944 | tf_op jit(solution)/shard_map/reduce_scatter | solution.py:730
  131.9 2.5 copy-start.9
  134.4 4.5 %copy-start.13 = (bf16[768,256]{1,0:T(8,128)(2,1)}, bf16[768,256]{1,0:T(8,128)(2,1)S(1)}, u32[]{:S(2)}) copy-start(bf16[768,256]{1,0:T(8,128)(2,1)S(1)} %get-tuple-element.40) | copy-start | bytes 1179652
  134.4 4.6 %copy-start.14 = (bf16[768,256]{1,0:T(8,128)(2,1)}, bf16[768,256]{1,0:T(8,128)(2,1)S(1)}, u32[]{:S(2)}) copy-start(bf16[768,256]{1,0:T(8,128)(2,1)S(1)} %get-tuple-element.41) | copy-start | bytes 1179652
  134.4 4.6 %copy-start.15 = (bf16[768,256]{1,0:T(8,128)(2,1)}, bf16[768,256]{1,0:T(8,128)(2,1)S(1)}, u32[]{:S(2)}) copy-start(bf16[768,256]{1,0:T(8,128)(2,1)S(1)} %get-tuple-element.42) | copy-start | bytes 1179652
  134.4 5.9 %copy-start.4 = (bf16[1,16,48,1024]{3,2,1,0:T(8,128)(2,1)S(1)}, bf16[1,16,48,1024]{3,2,1,0:T(8,128)(2,1)}, u32[]{:S(2)}) copy-start(bf16[1,16,48,1024]{3,2,1,0:T(8,128)(2,1)} %get-tuple-element.28) | copy-start | bytes 4718596
  134.5 5.9 %copy-start.6 = (bf16[1,16,48,1024]{3,2,1,0:T(8,128)(2,1)S(1)}, bf16[1,16,48,1024]{3,2,1,0:T(8,128)(2,1)}, u32[]{:S(2)}) copy-start(bf16[1,16,48,1024]{3,2,1,0:T(8,128)(2,1)} %get-tuple-element.29) | copy-start | bytes 4718596
  139.0 1.4 copy-start.16
  144.9 1.4 copy-start.5
  144.9 1.9 copy-start.7
  144.9 122.3 %reduce-scatter.6.cloned.1.call-start = ((), (), s32[]{:S(2)}) async-start(), calls=%async_computation.4 | async-start | bytes 3538944 | tf_op jit(solution)/shard_map/reduce_scatter | solution.py:731
  153.0 1.9 copy-start.1
  154.9 4.5 %copy-start.2 = (bf16[1,2048,768]{2,1,0:T(8,128)(2,1)S(1)}, bf16[1,2048,768]{2,1,0:T(8,128)(2,1)}, u32[]{:S(2)}) copy-start(bf16[1,2048,768]{2,1,0:T(8,128)(2,1)} %param.12) | copy-start | bytes 9437188
  154.9 4.5 %copy-start.11 = (bf16[768,256]{1,0:T(8,128)(2,1)S(1)}, bf16[768,256]{1,0:T(8,128)(2,1)}, u32[]{:S(2)}) copy-start(bf16[768,256]{1,0:T(8,128)(2,1)} %get-tuple-element.44) | copy-start | bytes 1179652
  154.9 4.5 %copy-start.12 = (bf16[768,256]{1,0:T(8,128)(2,1)S(1)}, bf16[768,256]{1,0:T(8,128)(2,1)}, u32[]{:S(2)}) copy-start(bf16[768,256]{1,0:T(8,128)(2,1)} %get-tuple-element.45) | copy-start | bytes 1179652
  154.9 4.5 %copy-start.17 = (f32[768,768]{1,0:T(8,128)S(1)}, f32[768,768]{1,0:T(8,128)}, u32[]{:S(2)}) copy-start(f32[768,768]{1,0:T(8,128)} %copy-done.16) | copy-start | bytes 7077892
Sparse Core Ops, SparseCore 0:
  131.8 35.2 reduce-scatter.7
  170.3 37.5 reduce-scatter.3
  211.0 37.8 reduce-scatter.5

commit v3 on v2

--- a/solution.py
+++ b/solution.py
@@ -414,12 +414,22 @@
 def return_kernel(
     cap,
     prod_ref,
-    drow_ref,
+    rows_ref,
+    grad_ref,
     picked_ref,
+    hid_ref,
+    dga_ref,
+    act_ref,
+    wg_ref,
+    wu_ref,
+    wd_ref,
     meta_ref,
     out_ref,
     dtok_ref,
     dcomb_ref,
+    dwg_ref,
+    dwu_ref,
+    dwd_ref,
     q,
     relay,
     part,
@@ -428,6 +438,16 @@
     stmat,
     dacc,
     dland,
+    rows,
+    grad,
+    wd,
+    hid,
+    dga,
+    act,
+    big,
+    drow,
+    lc,
+    ly,
     zs,
     zr,
     ds_,
@@ -437,15 +457,51 @@
     rs,
     rr,
     ls,
+    ws,
+    cs,
+    cr,
+    ys,
+    yr,
 ):
     tokens, features = out_ref.shape
     hd = features // 2
     per = 2 * cap
     sub = tokens // SUBS
+    chunks, dch, ff = big.shape[1:]
+    ft = ff // 3
     x, z, zp, zm, xp, xm = neighbours()
     zdev = (zp, zm)
-    srcs = (prod_ref, drow_ref)
-    greet((zp, zm, xp, xm))
+    dp = lax.axis_index("dp")
+    y, core = dp // 2, dp % 2
+    ny = chunks // 2
+    ydev = (((y + 1) % ny) * 2 + core, ((y + ny - 1) % ny) * 2 + core)
+    partner = 2 * y + 1 - core
+
+    loads = [
+        (grad_ref, grad),
+        (wd_ref.at[:, pl.ds(0, hd)], wd.at[0]),
+        (wd_ref.at[:, pl.ds(hd, hd)], wd.at[1]),
+        (dga_ref, dga),
+        (act_ref, act),
+        (wg_ref, big.at[0]),
+        (wu_ref, big.at[1]),
+        (rows_ref, rows),
+        (hid_ref, hid),
+        (picked_ref, wd),
+    ]
+
+    def load(i):
+        return pltpu.make_async_copy(*loads[i], ws.at[i])
+
+    for i in range(9):
+        load(i).start()
+
+    barrier = pltpu.get_barrier_semaphore()
+    for d in (zp, zm, xp, xm):
+        pl.semaphore_signal(barrier, inc=1, device_id={"expert": d}, device_id_type=MESH)
+    for d in (partner, *ydev):
+        pl.semaphore_signal(barrier, inc=1, device_id={"dp": d}, device_id_type=MESH)
+    pl.semaphore_wait(barrier, 7)
 
     def where_at(t):
         st, j = t // 8, t % 8
@@ -478,6 +534,8 @@
             src.at[h, p * 4 + 3], q.at[st, h, p, pl.ds(3 * per, per), :], ls.at[st, h, p]
         )
 
+    srcs = (prod_ref, drow)
+
     def send(t):
         st, _, h, p = where_at(t)
         for i in range(2):
@@ -490,7 +548,7 @@
 
     def forward(t):
         st, _, h, p = where_at(t)
-        xcopy(st, h, p, 0, prod_ref).wait_recv()
+        xcopy(st, h, p, 0, drow).wait_recv()
         fcopy(st, h, p).start()
 
     def chunk(h, s):
@@ -522,11 +580,11 @@
     def scatter(t):
         st, _, h, p = where_at(t)
         for k in (1, 2):
-            xcopy(st, h, p, k, prod_ref).wait_recv()
+            xcopy(st, h, p, k, drow).wait_recv()
         fcopy(st, h, p).wait_recv()
-        own(st, h, p, prod_ref).wait()
-        rows = pl.ds(pl.multiple_of(p * 2 * tokens, 2 * tokens), 2 * tokens)
-        part[st, h, rows, :] = jnp.dot(
+        own(st, h, p, drow).wait()
+        at = pl.ds(pl.multiple_of(p * 2 * tokens, 2 * tokens), 2 * tokens)
+        part[st, h, at, :] = jnp.dot(
             stmat[st, p], q[st, h, p], preferred_element_type=F32
         ).astype(BF)
 
@@ -534,18 +592,18 @@
         for u in us:
             for h in range(2):
                 m = chunk(h, s + 1)
-                rows = pl.ds(pl.multiple_of(m * tokens + sub * u, sub), sub)
+                at = pl.ds(pl.multiple_of(m * tokens + sub * u, sub), sub)
                 zcopy(st, h, s, u).wait_recv()
-                part[st, h, rows, :] += land[st, h, s, pl.ds(sub * u, sub), :]
+                part[st, h, at, :] += land[st, h, s, pl.ds(sub * u, sub), :]
                 zcopy(st, h, s + 1, u).start()
 
     def finish(st, us):
         out = (out_ref, dtok_ref)[st]
         for u in us:
-            rows = pl.ds(sub * u, sub)
+            at = pl.ds(sub * u, sub)
             for h in range(2):
                 zcopy(st, h, NZ - 2, u).wait_recv()
-                out[rows, h * hd : (h + 1) * hd] = part[st, h, rows, :] + land[st, h, NZ - 2, rows, :]
+                out[at, h * hd : (h + 1) * hd] = part[st, h, at, :] + land[st, h, NZ - 2, at, :]
 
     def weights(p):
         meta = meta_of(p)
@@ -553,8 +611,9 @@
         for blk in range(NX):
             v = jnp.zeros((per, 1), F32)
             for h in range(2):
+                at = pl.ds(pl.multiple_of(p * 4 * per + blk * per, per), per)
                 a = q[0, h, p, blk * per : (blk + 1) * per, :].astype(F32)
-                b = picked_ref[h, p, blk * per : (blk + 1) * per, :].astype(F32)
+                b = wd[h, at, :].astype(F32)
                 v = v + jnp.sum(a * b, axis=1, keepdims=True)
             hit = row_masks(meta, x, z, cap, blk)
             w = sum(jnp.where(hit[k], meta[4 + k : 5 + k, :], 0.0) for k in range(4))
@@ -568,16 +627,127 @@
         for i in range(2):
             dacc[2 * p + i, 4:8, :] = jnp.zeros((4, tokens), F32)
 
+    def nt(a, b):
+        return lax.dot_general(a, b, (((1,), (1,)), ((), ())), preferred_element_type=F32)
+
+    def hidden_tile(f):
+        dh = nt(grad[0], wd[0, f * ft : (f + 1) * ft, :]) + nt(grad[1], wd[1, f * ft : (f + 1) * ft, :])
+        dga[f] = (dh * dga[f].astype(F32)).astype(BF)
+        act[f] = (dh * act[f].astype(F32)).astype(BF)
+
+    def row_tile(n):
+        out = sum(
+            nt(dga[f], big[0, n, :, f * ft : (f + 1) * ft])
+            + nt(act[f], big[1, n, :, f * ft : (f + 1) * ft])
+            for f in range(3)
+        )
+        lanes = pl.ds(pl.multiple_of((n % 4) * dch, dch), dch)
+        drow[n // 4, :, :, lanes] = out.astype(BF).reshape(16, per, dch)
+
+    def target(k):
+        return (y + jnp.where(k == 0, ny - 1, jnp.where(k == 3, 0, k))) % ny
+
+    def grad_chunk(c):
+        lanes = pl.ds(pl.multiple_of((c % 4) * dch, dch), dch)
+        a = rows[c // 4, :, lanes].T
+        b = grad[c // 4, :, lanes].T
+        for i, (lhs, rhs) in enumerate(((a, dga), (a, act), (b, hid))):
+            for f in range(3):
+                big[i, c, :, f * ft : (f + 1) * ft] = jnp.dot(
+                    lhs, rhs[f], preferred_element_type=F32
+                ).astype(BF)
+
+    def dpcopy(src, dst, send, recv, dev):
+        return pltpu.make_async_remote_copy(
+            src_ref=src,
+            dst_ref=dst,
+            send_sem=send,
+            recv_sem=recv,
+            device_id={"dp": dev},
+            device_id_type=MESH,
+        )
+
+    def ccopy(k):
+        return dpcopy(big.at[:, 2 * target(k) + 1 - core], lc.at[k], cs.at[k], cr.at[k], partner)
+
+    half = dch // 2
+
+    def ycopy(i, s, g):
+        a = (y + 2 * ny - 1 - s) % ny if i == 0 else (y + 1 + s) % ny
+        src = big.at[g, 2 * a + core, pl.ds(half * i, half), :]
+        return dpcopy(src, ly.at[i, s, g], ys.at[i, s, g], yr.at[i, s, g], ydev[i])
+
+    def grad_piece(k):
+        mine = (k >= 4).astype(jnp.int32)
+        kk = k - 4 * mine
+        c = 2 * target(kk) + jnp.where(k >= 4, core, 1 - core)
+        grad_chunk(c)
+
+        @pl.when(k < 4)
+        def _():
+            ccopy(kk).start()
+
+        @pl.when(k >= 4)
+        def _():
+            ccopy(kk).wait_recv()
+            for i in range(3):
+                big[i, c] += lc[kk, i]
+
+            for i in range(2):
+
+                @pl.when(kk == i)
+                def _():
+                    for g in range(3):
+                        ycopy(i, 0, g).start()
+
+    def dp_ring(n):
+        s, g = n // 3, n % 3
+        for i in range(2):
+            b = (y + 2 * ny - 2 - s) % ny if i == 0 else (y + 2 + s) % ny
+            ycopy(i, s, g).wait_recv()
+            big[g, 2 * b + core, half * i : half * (i + 1), :] += ly[i, s, g]
+
+            @pl.when(s < ny - 2)
+            def _():
+                ycopy(i, s + 1, g).start()
+
+    def piece(slot):
+        @pl.when(slot == 0)
+        def _():
+            hidden_tile(2)
+            for i in (5, 6):
+                load(i).wait()
+
+        @pl.when((slot >= 1) & (slot < 9))
+        def _():
+            row_tile(slot - 1)
+
+        @pl.when(slot == 2)
+        def _():
+            for i in (7, 8):
+                load(i).wait()
+            load(9).start()
+
+        @pl.when((slot >= 9) & (slot < 17))
+        def _():
+            grad_piece(slot - 9)
+
+        n = ((slot - 17) * 2 + 2) // 3
+
+        @pl.when((slot >= 17) & (slot < 30) & ((slot - 17) % 3 != 2))
+        def _():
+            dp_ring(n)
+
     send(0)
     send(1)
     mats(0)
+    for i in range(5):
+        load(i).wait()
+    hidden_tile(0)
     forward(0)
     send(2)
-
-    @pl.loop(1, 4)
-    def _(p):
-        mats(p)
-
+    mats(3)
+    hidden_tile(1)
     forward(1)
 
     @pl.loop(0, 16)
@@ -590,18 +760,6 @@
 
         scatter(t)
 
-        @pl.when(j >= 2)
-        def _():
-            ring(st, j - 2, range(0, SUBS // 2))
-
-        @pl.when(t + 2 < 16)
-        def _():
-            forward(t + 2)
-
-        @pl.when(j >= 2)
-        def _():
-            ring(st, j - 2, range(SUBS // 2, SUBS))
-
         @pl.when(j < 2)
         def _():
             for u in range(SUBS):
@@ -611,16 +769,37 @@
                     def _():
                         zcopy(st, hh, 0, u).start()
 
+        @pl.when(j >= 2)
+        def _():
+            ring(st, j - 2, range(0, SUBS // 2))
+
+        @pl.when(t < 2)
+        def _():
+            mats(t + 1)
+
+        piece(2 * t)
+
+        @pl.when(t + 2 < 16)
+        def _():
+            forward(t + 2)
+
+        @pl.when(j >= 2)
+        def _():
+            ring(st, j - 2, range(SUBS // 2, SUBS))
+
+        piece(2 * t + 1)
+
         @pl.when(t == 9)
         def _():
             finish(0, range(SUBS))
+            load(9).wait()
+
+        @pl.when((t == 9) | (t == 10) | (t == 12) | (t == 14))
+        def _():
+            weights((t - 8) // 2)
 
         @pl.when(t == 9)
         def _():
-            @pl.loop(0, 4)
-            def _(i):
-                weights(i)
-
             dcopy(0).start()
 
         @pl.when(t >= 10)
@@ -630,6 +809,9 @@
             dacc[s + 2] += dland[s]
             dcopy(s + 1).start()
 
+    for g, out in enumerate((dwg_ref, dwu_ref)):
+        out[...] = big[g, dp]
+    dwd_ref[...] = big[2, dp].T
     finish(1, range(SUBS))
     dcopy(NZ - 2).wait_recv()
     dcomb_ref[...] = dacc[0] + dland[NZ - 2]
@@ -646,30 +828,48 @@
         @pl.loop(0, 8)
         def _(i):
             for k in range(3):
-                xcopy(st, i // 4, i % 4, k, prod_ref).wait_send()
+                xcopy(st, i // 4, i % 4, k, drow).wait_send()
             fcopy(st, i // 4, i % 4).wait_send()
 
     @pl.loop(0, NZ - 1)
     def _(s):
         dcopy(s).wait_send()
 
-
-def give_back(produced, d_rows, picked, meta, tokens, cap):
-    features = 2 * produced.shape[3]
+    @pl.loop(0, 4)
+    def _(k):
+        ccopy(k).wait_send()
+
+    @pl.loop(0, 9)
+    def _(n):
+        for i in range(2):
+            ycopy(i, n // 3, n % 3).wait_send()
+
+
+def give_back(produced, rows, grad, picked, hid, dga, act, w_gate, w_up, w_down, meta, tokens, cap):
+    features, ff = w_gate.shape
     hd = features // 2
     per = 2 * cap
+    n_rows = 16 * per
+    ndp = lax.axis_size("dp")
+    dch = features // ndp
+    ny = ndp // 2
     dma = pltpu.SemaphoreType.DMA
     vmem = pl.BlockSpec(memory_space=pltpu.VMEM)
     hbm = pl.BlockSpec(memory_space=pl.ANY)
+    share = jax.ShapeDtypeStruct((dch, ff), BF)
+    flat = (2, n_rows, hd)
     return pl.pallas_call(
         functools.partial(return_kernel, cap),
         out_shape=(
             jax.ShapeDtypeStruct((tokens, features), BF),
             jax.ShapeDtypeStruct((tokens, features), BF),
             jax.ShapeDtypeStruct((8, tokens), F32),
+            share,
+            share,
+            jax.ShapeDtypeStruct((ff, dch), BF),
         ),
-        in_specs=[hbm, hbm, vmem, vmem],
-        out_specs=(vmem,) * 3,
+        in_specs=[hbm] * 10 + [vmem],
+        out_specs=(vmem,) * 6,
         scratch_shapes=[
             pltpu.VMEM((2, 2, 4, 4 * per, hd), BF),
             pltpu.VMEM((2, 2, 4, per, hd), BF),
@@ -679,6 +879,16 @@
             pltpu.VMEM((2, 4, 2 * tokens, 4 * per), BF),
             pltpu.VMEM((NZ, 8, tokens), F32),
             pltpu.VMEM((NZ - 1, 8, tokens), F32),
+            pltpu.VMEM(flat, BF),
+            pltpu.VMEM(flat, BF),
+            pltpu.VMEM((2, ff, hd), BF),
+            pltpu.VMEM(hid.shape, BF),
+            pltpu.VMEM(hid.shape, BF),
+            pltpu.VMEM(hid.shape, BF),
+            pltpu.VMEM((3, ndp, dch, ff), BF),
+            pltpu.VMEM((2, 16, per, hd), BF),
+            pltpu.VMEM((4, 3, dch, ff), BF),
+            pltpu.VMEM((2, ny - 1, 3, dch // 2, ff), BF),
             dma((2, 2, NZ - 1, SUBS)),
             dma((2, 2, NZ - 1, SUBS)),
             dma((NZ - 1,)),
@@ -688,50 +898,45 @@
             dma((2, 2, 4)),
             dma((2, 2, 4)),
             dma((2, 2, 4)),
+            dma((10,)),
+            dma((4,)),
+            dma((4,)),
+            dma((2, ny - 1, 3)),
+            dma((2, ny - 1, 3)),
         ],
         compiler_params=pltpu.CompilerParams(
-            collective_id=1, has_side_effects=True, vmem_limit_bytes=62 * 1024 * 1024
+            collective_id=1, has_side_effects=True, vmem_limit_bytes=67043328
         ),
         name="give_back",
-    )(produced, d_rows, picked, meta)
+    )(
+        produced,
+        rows.reshape(flat),
+        grad.reshape(flat),
+        picked.reshape(flat),
+        hid,
+        dga,
+        act,
+        w_gate.reshape(ndp, dch, ff),
+        w_up.reshape(ndp, dch, ff),
+        w_down,
+        meta,
+    )
 
 
 def per_device(tokens, routes, combine, cotangent, w_gate, w_up, w_down):
-    n, features = tokens.shape
+    n = tokens.shape[0]
     per_token = routes.shape[1]
     experts = w_gate.shape[0] * lax.axis_size("expert")
     cap = 3 * n * per_token // (2 * experts)
-    per = 2 * cap
     rc = jnp.concatenate([routes.T.astype(F32), combine.T], axis=0)
     w_gate, w_up, w_down = w_gate[0], w_up[0], w_down[0]
-    rows2, grad2, picked, meta, hid3, dga3, act3, produced = dispatch(
+    rows, grad, picked, meta, hid, dga, act, produced = dispatch(
         tokens, cotangent, rc, w_gate, w_up, w_down, cap
     )
-
-    def whole(a):
-        return jnp.concatenate([a[0], a[1]], axis=-1).reshape(16 * per, features)
-
-    def wide(a):
-        return jnp.concatenate([a[0], a[1], a[2]], axis=-1)
-
-    rows, d_in = whole(rows2), whole(grad2)
-    hidden = wide(hid3)
-    d_hidden = jnp.dot(d_in, w_down.T, preferred_element_type=F32)
-    d_gate = (d_hidden * wide(dga3).astype(F32)).astype(BF)
-    d_up = (d_hidden * wide(act3).astype(F32)).astype(BF)
-    d_rows = (
-        jnp.dot(d_gate, w_gate.T, preferred_element_type=F32)
-        + jnp.dot(d_up, w_up.T, preferred_element_type=F32)
-    ).astype(BF)
-    d_rows = jnp.stack([d_rows[:, : features // 2], d_rows[:, features // 2 :]]).reshape(produced.shape)
-    part_down = jnp.dot(hidden.T, d_in, preferred_element_type=F32).astype(BF)
-    part_gate = jnp.dot(rows.T, d_gate, preferred_element_type=F32).astype(BF)
-    part_up = jnp.dot(rows.T, d_up, preferred_element_type=F32).astype(BF)
-    d_w_gate = lax.psum_scatter(part_gate[None], "dp", scatter_dimension=1, tiled=True)
-    d_w_up = lax.psum_scatter(part_up[None], "dp", scatter_dimension=1, tiled=True)
-    d_w_down = lax.psum_scatter(part_down[None], "dp", scatter_dimension=2, tiled=True)
-    output, d_tokens, d_comb = give_back(produced, d_rows, picked, meta, n, cap)
-    return output, d_tokens, d_comb[:per_token].T, d_w_gate, d_w_up, d_w_down
+    output, d_tokens, d_comb, d_w_gate, d_w_up, d_w_down = give_back(
+        produced, rows, grad, picked, hid, dga, act, w_gate, w_up, w_down, meta, n, cap
+    )
+    return output, d_tokens, d_comb[:per_token].T, d_w_gate[None], d_w_up[None], d_w_down[None]
 
 
 def solution(mesh):

time: 278 us -> 228 us (0.82)
  matrix products: 26.7 us -> 0 us
  between operations: 13.9 us -> 0.67 us
  local copies, waits for them, and re-layouts: 21.5 us -> 8.36 us
  Pallas kernels: 211 us -> 216 us
    dot_general x6 -> x0, matrix products: 26.7 us -> none  [the longest x1 6.19 us: per_device(): part_up = jnp.dot(rows.T, d_up, preferred_element_type=F32).astype(BF)]
    pallas_call x1, Pallas kernels: 101 us -> 107 us  [give_back(): pl.pallas_call(functools.partial(return_kernel, cap), out_shape=(jax.Shap...]
    slice x2 -> x0, local copies, waits for them, and re-layouts: 4.68 us -> none  [the longest x1 4.31 us: whole(): return jnp.concatenate([a[0], a[1]], axis=-1).reshape(16 * per, features)]
    unnamed x38 -> x9, local copies, waits for them, and re-layouts: 11.4 us -> 7.03 us
    squeeze x2 -> x0, local copies, waits for them, and re-layouts: 4.22 us -> none  [wide(): return jnp.concatenate([a[0], a[1], a[2]], axis=-1)]
  transfers between devices with their start and end apart: 3 -> 0, of which waited for: 0 -> 0; matrix products, arithmetic and copies ran while one was open for 10% -> 0% of each run, Pallas kernels for 37% -> 0%
where the time goes in v3:
time: 228 us; the launch traced here: 227 us
  Pallas kernels  216 us (95%)
  local copies, waits for them, and re-layouts  8.36 us (4%)
    pallas_call x1, Pallas kernels, dispatch(): pl.pallas_call(functools.partial(dispatch_kernel, cap), out_shape=(halves...  110 us
    pallas_call x1, Pallas kernels, give_back(): pl.pallas_call(functools.partial(return_kernel, cap), out_shape=(jax.Shap...  107 us
    unnamed x9, local copies, waits for them, and re-layouts  7.03 us

profile of v3, /device:TPU:8, one launch (start us, length us, event | category | flops | bytes accessed | tf_op | source)
XLA Modules:
  0.0 227.2 jit_solution(3426705905312632570)
XLA Ops:
  0.6 0.7 convert_bitcast_fusion
  1.3 1.3 pad_maximum_fusion.rc_ref
  2.6 109.6 %dispatch.1 = (bf16[2,16,48,1024]{3,2,1,0:T(8,128)(2,1)}, bf16[2,16,48,1024]{3,2,1,0:T(8,128)(2,1)}, bf16[2,4,192,1024]{3,2,1,0:T(8,128)(2,1)}, f32[8,8,128]{2,1...) custom-call(bf16[128,2048]{1,0:T(8,128)(2,1)} %tok_ref.1, ...), custom_call_target="tpu_custom_call" | custom-call | tf_op jit(solution)/shard_map/dispatch/pallas_call | solution.py:365
  112.2 106.7 %give_back.1 = (bf16[128,2048]{1,0:T(8,128)(2,1)}, bf16[128,2048]{1,0:T(8,128)(2,1)}, f32[8,128]{1,0:T(8,128)}, bf16[256,768]{1,0:T(8,128)(2,1)}, bf16[256,768]{1,0:T(8,128)(2,1)}, /*index=5*/bf16[768,256]{1,0:T(8,128)(2,1)}) custom-call(bf16[2,16,48,1024]{3,2,1,0:T(8,128)(2,1)} %get-tuple-element.20.prod_ref, bf16[2,768,1024]{2,1,0:T(8,128)(2,1)} %bitcast.22, ...), custom_call_target="tpu_custom_call" | custom-call | tf_op jit(solution)/shard_map/give_back/pallas_call | solution.py:861
  218.9 0.0 copy-start.1
  218.9 0.0 copy-start
  218.9 1.3 slice_bitcast_fusion
  220.2 1.9 copy.18
  222.1 1.9 copy.19
  224.0 1.8 copy.20
  225.7 0.0 copy-done.1
  225.7 0.7 copy.21
  226.5 0.0 copy-done
  226.5 0.7 copy.22
Async XLA Ops:
  218.9 6.9 %copy-start.1 = (bf16[256,768]{1,0:T(8,128)(2,1)S(1)}, bf16[256,768]{1,0:T(8,128)(2,1)}, u32[]{:S(2)}) copy-start(bf16[256,768]{1,0:T(8,128)(2,1)} %get-tuple-element.32) | copy-start | bytes 1179652
  218.9 7.6 %copy-start = (bf16[768,256]{1,0:T(8,128)(2,1)S(1)}, bf16[768,256]{1,0:T(8,128)(2,1)}, u32[]{:S(2)}) copy-start(bf16[768,256]{1,0:T(8,128)(2,1)} %get-tuple-element.33) | copy-start | bytes 1179652

commit v4 on v0

v4 whole, which is shorter than its diff:
```python
import functools

import jax
import jax.numpy as jnp
from jax import lax
from jax.experimental import pallas as pl
from jax.experimental.pallas import tpu as pltpu
from jax.sharding import PartitionSpec as P

MESH = pl.DeviceIdType.MESH
NZ = 8
NX = 4
SUBS = 4
BF = jnp.bfloat16
F32 = jnp.float32


def neighbours():
    e = lax.axis_index("expert")
    x, z = e // NZ, e % NZ
    zp = x * NZ + (z + 1) % NZ
    zm = x * NZ + (z + NZ - 1) % NZ
    xp = ((x + 1) % NX) * NZ + z
    xm = ((x + NX - 1) % NX) * NZ + z
    return x, z, zp, zm, xp, xm


def rcopy(src, dst, send, recv, dev):
    return pltpu.make_async_remote_copy(
        src_ref=src,
        dst_ref=dst,
        send_sem=send,
        recv_sem=recv,
        device_id={"expert": dev},
        device_id_type=MESH,
    )


def row_masks(meta, x, z, cap, blk):
    width = meta.shape[1]
    per = 2 * cap
    col = lax.broadcasted_iota(jnp.int32, (per, width), 1)
    row = lax.broadcasted_iota(jnp.int32, (per, width), 0)
    second = (row >= cap).astype(jnp.int32)
    shift = (col[0:1] >= width // 2).astype(jnp.int32) * 4096
    expert = ((x + blk + 1) % NX) * NZ + z
    ids = row - cap * second + 4096 * second + expert * cap
    return [ids == (meta[k : k + 1, :].astype(jnp.int32) + shift) for k in range(4)]


def layer_kernel(
    cap,
    tok_ref,
    cot_ref,
    routes_ref,
    combine_ref,
    wg_ref,
    wu_ref,
    wd_ref,
    out_ref,
    dtok_ref,
    dcomb_ref,
    dwg_ref,
    dwu_ref,
    dwd_ref,
    ag,
    sx,
    r,
    relay,
    q,
    land,
    big,
    wd,
    gate,
    hid,
    dga,
    act,
    prod,
    lc,
    ly,
    metab,
    smat,
    cmat,
    smatf,
    stmat,
    dacc,
    dland,
    zs,
    zr,
    ms,
    mr,
    xs,
    xr,
    rs,
    rr,
    ls,
    ws,
    os_,
    ds_,
    dr,
    cs,
    cr,
    ys,
    yr,
    free,
):
    tokens, features = tok_ref.shape
    ff = wg_ref.shape[1]
    hd = features // 2
    per = 2 * cap
    sub = tokens // SUBS
    ft, nt = ff // 3, features // 4
    x, z, zp, zm, xp, xm = neighbours()
    zdev = (zp, zm)
    dp = lax.axis_index("dp")
    y, core = dp // 2, dp % 2
    chunks = lax.axis_size("dp")
    ny = chunks // 2
    dch = features // chunks
    half = dch // 2
    ydev = (((y + 1) % ny) * 2 + core, ((y + ny - 1) % ny) * 2 + core)
    partner = 2 * y + 1 - core

    def rows_at(n, size):
        return pl.ds(pl.multiple_of(n * size, size), size)

    loads = [
        (tok_ref.at[:, pl.ds(0, hd)], ag.at[0, 0, pl.ds(0, tokens), :]),
        (tok_ref.at[:, pl.ds(hd, hd)], ag.at[0, 1, pl.ds(0, tokens), :]),
        (cot_ref.at[:, pl.ds(0, hd)], ag.at[1, 0, pl.ds(0, tokens), :]),
        (cot_ref.at[:, pl.ds(hd, hd)], ag.at[1, 1, pl.ds(0, tokens), :]),
        (wg_ref, big.at[0]),
        (wu_ref, big.at[1]),
        (wd_ref.at[:, pl.ds(0, hd)], wd.at[0]),
        (wd_ref.at[:, pl.ds(hd, hd)], wd.at[1]),
    ]

    def load(i):
        return pltpu.make_async_copy(*loads[i], ws.at[i])

    for i in range(4):
        load(i).start()

    barrier = pltpu.get_barrier_semaphore()
    for d in (zp, zm, xp, xm):
        pl.semaphore_signal(barrier, inc=1, device_id={"expert": d}, device_id_type=MESH)
    for d in (partner, *ydev):
        pl.semaphore_signal(barrier, inc=1, device_id={"dp": d}, device_id_type=MESH)
    pl.semaphore_wait(barrier, 7)

    def where_at(t):
        st, j = t // 8, t % 8
        h = j % 2
        return st, j, h, jnp.where(h == 0, j // 2, 3 - j // 2)


    def zout(st, h, s, u):
        a = s if h == 0 else (NZ - s) % NZ
        b = s + 1 if h == 0 else NZ - 1 - s
        src = ag.at[st, h, pl.ds(pl.multiple_of(a * tokens + sub * u, sub), sub), :]
        dst = ag.at[st, h, pl.ds(pl.multiple_of(b * tokens + sub * u, sub), sub), :]
        return rcopy(src, dst, zs.at[st, h, s, u], zr.at[st, h, s, u], zdev[h])

    def mcopy(h, s):
        a = s if h == 0 else (NZ - s) % NZ
        b = s + 1 if h == 0 else NZ - 1 - s
        return rcopy(metab.at[a], metab.at[b], ms.at[h, s], mr.at[h, s], zdev[h])

    def xout(st, h, p, i):
        far = jnp.where(h == 0, xp, xm)
        dst = relay.at[st, h, p] if i == 0 else r.at[st, h, rows_at(p * 4 + i - 1, per), :]
        return rcopy(
            sx.at[st, h, p, pl.ds((1, 0, 2)[i] * per, per), :],
            dst,
            xs.at[st, h, p, i],
            xr.at[st, h, p, i],
            (far, xp, xm)[i],
        )

    def fout(st, h, p):
        far = jnp.where(h == 0, xp, xm)
        return rcopy(
            relay.at[st, h, p],
            r.at[st, h, rows_at(p * 4 + 2, per), :],
            rs.at[st, h, p],
            rr.at[st, h, p],
            far,
        )


    def xback(st, h, p, i, src):
        far = jnp.where(h == 0, xp, xm)
        dst = relay.at[st, h, p] if i == 0 else q.at[st - 2, h, p, pl.ds((0, 2)[i - 1] * per, per), :]
        return rcopy(
            src.at[h, p, pl.ds((2, 0, 1)[i] * per, per), :],
            dst,
            xs.at[st, h, p, i],
            xr.at[st, h, p, i],
            (far, xm, xp)[i],
        )

    def fback(st, h, p):
        far = jnp.where(h == 0, xp, xm)
        return rcopy(
            relay.at[st, h, p],
            q.at[st - 2, h, p, pl.ds(per, per), :],
            rs.at[st, h, p],
            rr.at[st, h, p],
            far,
        )

    drow = sx.at[0]
    srcs = (prod, drow)

    def own(st, h, p, src):
        return pltpu.make_async_copy(
            src.at[h, p, pl.ds(3 * per, per), :],
            q.at[st - 2, h, p, pl.ds(3 * per, per), :],
            ls.at[st - 2, h, p],
        )

    def chunk(h, s):
        return s + 1 if h == 0 else NZ - 1 - s

    def zback(st, h, s, u):
        m = chunk(h, s)
        src = ag.at[st - 2, h, pl.ds(pl.multiple_of(m * tokens + sub * u, sub), sub), :]
        dst = land.at[h, s, pl.ds(sub * u, sub), :]
        return rcopy(src, dst, zs.at[st, h, s, u], zr.at[st, h, s, u], zdev[h])

    def dcopy(s):
        return rcopy(dacc.at[s + 1], dland.at[s], ds_.at[s], dr.at[s], zp)


    def dpcopy(src, dst, send, recv, dev):
        return pltpu.make_async_remote_copy(
            src_ref=src,
            dst_ref=dst,
            send_sem=send,
            recv_sem=recv,
            device_id={"dp": dev},
            device_id_type=MESH,
        )

    def target(k):
        return (y + jnp.where(k == 0, ny - 1, jnp.where(k == 3, 0, k))) % ny

    def ccopy(k):
        src = big.at[:, rows_at(2 * target(k) + 1 - core, dch), :]
        return dpcopy(src, lc.at[k], cs.at[k], cr.at[k], partner)

    def ycopy(i, s, g):
        a = (y + 2 * ny - 1 - s) % ny if i == 0 else (y + 1 + s) % ny
        src = big.at[g, rows_at(2 * (2 * a + core) + i, half), :]
        return dpcopy(src, ly.at[i, s, g], ys.at[i, s, g], yr.at[i, s, g], ydev[i])


    for h in range(2):
        load(h).wait()
        for u in range(SUBS):
            zout(0, h, 0, u).start()
    for i in range(4, 8):
        load(i).start()

    experts = NX * NZ
    names = [routes_ref[k : k + 1, :] for k in range(4)]
    ids = lax.broadcasted_iota(jnp.int32, (experts, tokens), 0)
    hits = [ids == n for n in names]
    count = sum(hit.astype(F32) for hit in hits)
    earlier = lax.broadcasted_iota(jnp.int32, (tokens, tokens), 0)
    later = lax.broadcasted_iota(jnp.int32, (tokens, tokens), 1)
    before = jnp.dot(
        count.astype(BF), (earlier < later).astype(F32).astype(BF), preferred_element_type=F32
    )
    for k in range(4):
        slot = jnp.sum(jnp.where(hits[k], before, 0.0), axis=0, keepdims=True)
        metab[0, k : k + 1, :] = names[k].astype(F32) * cap + slot
        metab[0, 4 + k : 5 + k, :] = combine_ref[k : k + 1, :]
    for h in range(2):
        mcopy(h, 0).start()
    for i in range(2, 4):
        load(i).wait()

    cmat[...] = jnp.zeros_like(cmat)

    def meta_of(p):
        return jnp.concatenate([metab[2 * p], metab[2 * p + 1]], axis=1)

    def masks(p):
        meta = meta_of(p)
        for blk in range(NX):
            at = pl.ds(blk * per, per)
            hit = row_masks(meta, x, z, cap, blk)
            one = functools.reduce(jnp.logical_or, hit).astype(F32)
            weight = sum(jnp.where(hit[k], meta[4 + k : 5 + k, :], 0.0) for k in range(4))
            smatf[at, :] = weight
            smat[p, at, :] = one.astype(BF)
            here = lax.broadcasted_iota(jnp.int32, (per, 128), 1) == p
            cmat[at, :] = jnp.where(here, jnp.sum(weight, axis=1, keepdims=True), cmat[at, :])
        stmat[0, p] = smatf[...].T.astype(BF)
        stmat[1, p] = smat[p].T

    def row_weights(p, at):
        size = cmat.shape[0] if at is None else per
        here = lax.broadcasted_iota(jnp.int32, (size, 128), 1) == p
        return jnp.sum(jnp.where(here, cmat[...] if at is None else cmat[at, :], 0.0), axis=1, keepdims=True)

    def forward_out(t):
        st, _, h, p = where_at(t)
        xout(st, h, p, 0).wait_recv()
        fout(st, h, p).start()

    def arrived(st):
        @pl.loop(0, 8)
        def _(i):
            h, p = i // 4, i % 4
            for k in (1, 2):
                xout(st, h, p, k).wait_recv()
            fout(st, h, p).wait_recv()

    def ring_out(t, u):
        st, j, _, _ = where_at(t)

        @pl.when(j < NZ - 1)
        def _():
            for h in range(2):
                zout(st, h, j, u).wait_recv()

                @pl.when(j < NZ - 2)
                def _():
                    zout(st, h, j + 1, u).start()

                @pl.when((j == NZ - 2) & (st == 0))
                def _():
                    zout(1, h, 0, u).start()

    def project(i, f):
        lanes = rows_at(f, ft)
        a = jnp.dot(r[0, 0], big[i, 0:hd, lanes], preferred_element_type=F32)
        return a + jnp.dot(r[0, 1], big[i, hd:, lanes], preferred_element_type=F32)

    def gate_tile(f):
        gate[...] = project(0, f)

    def up_tile(f):
        up = project(1, f)
        g = gate[...]
        sig = 1.0 / (1.0 + jnp.exp(-g))
        a = g * sig
        act[f] = a.astype(BF)
        hid[f] = (a * up).astype(BF)
        dga[f] = (up * sig * (1.0 + g * (1.0 - sig))).astype(BF)

    def down_tile(n):
        lanes = pl.ds((n % 2) * nt, nt)
        out = sum(
            jnp.dot(hid[f], wd[n // 2, f * ft : (f + 1) * ft, lanes], preferred_element_type=F32)
            for f in range(3)
        )
        prod[n // 2, :, :, lanes] = out.astype(BF).reshape(4, 4 * per, nt)

    def send(t):
        st, _, h, p = where_at(t)
        for i in range(2):

            @pl.when(st == i)
            def _():
                for k in range(3):
                    xback(2 + i, h, p, k, srcs[i]).start()
                own(2 + i, h, p, srcs[i]).start()

    def forward_back(t):
        st, _, h, p = where_at(t)
        xback(2 + st, h, p, 0, prod).wait_recv()
        fback(2 + st, h, p).start()

    @pl.loop(0, 16)
    def _(t):
        st, j, h, p = where_at(t)

        @pl.when(t == 14)
        def _():
            send(0)

        @pl.when(st == 0)
        def _():
            for hh, n in ((0, 4), (1, 3)):

                @pl.when(j < n)
                def _():
                    mcopy(hh, j).wait_recv()

                @pl.when(j + 1 < n)
                def _():
                    mcopy(hh, j + 1).start()

        for u in range(SUBS):
            ring_out(t, u)
            if u == 0:

                @pl.when(t == 10)
                def _():
                    arrived(0)
                    for i in range(4, 8):
                        load(i).wait()

                @pl.when((t >= 10) & (t < 13))
                def _():
                    gate_tile(t - 10)

            if u == 1:

                @pl.when(t > 0)
                def _():
                    forward_out(t - 1)

            if u == 2:

                @pl.when((t >= 10) & (t < 13))
                def _():
                    up_tile(t - 10)

            @pl.when(t == 13)
            def _():
                down_tile(u)

        @pl.when(t < 4)
        def _():
            masks(p)

        got = jnp.dot(
            smat[p], ag[st, h, rows_at(p, 2 * tokens), :], preferred_element_type=F32
        )
        got = (got * jnp.where(st == 1, row_weights(p, None), 1.0)).astype(BF)
        sx[st, h, p] = got
        r[st, h, rows_at(p * 4 + 3, per), :] = got[3 * per :]
        for i in range(3):
            xout(st, h, p, i).start()

        @pl.when(t == 15)
        def _():
            send(1)

    forward_out(15)
    forward_back(0)
    send(2)

    def sent_out(st):
        for h in range(2):

            @pl.loop(0, NZ - 1)
            def _(s):
                for u in range(SUBS):
                    zout(st, h, s, u).wait_send()

    def xsent_out(st):
        @pl.loop(0, 8)
        def _(i):
            for k in range(3):
                xout(st, i // 4, i % 4, k).wait_send()
            fout(st, i // 4, i % 4).wait_send()

    sent_out(0)
    xsent_out(0)
    forward_back(1)

    def scatter(t):
        st, _, h, p = where_at(t)
        for k in (1, 2):
            xback(2 + st, h, p, k, prod).wait_recv()
        fback(2 + st, h, p).wait_recv()
        own(2 + st, h, p, prod).wait()
        ag[st, h, rows_at(p, 2 * tokens), :] = jnp.dot(
            stmat[st, p], q[st, h, p], preferred_element_type=F32
        ).astype(BF)

    def upstream(h):
        return {"expert": zm if h == 0 else zp}

    def give_slot(h):
        pl.semaphore_signal(free.at[h], inc=1, device_id=upstream(h), device_id_type=MESH)

    def ring_back(st, s, u):
        for h in range(2):
            at = pl.ds(pl.multiple_of(chunk(h, s + 1) * tokens + sub * u, sub), sub)
            zback(2 + st, h, s, u).wait_recv()
            ag[st, h, at, :] += land[h, s, pl.ds(sub * u, sub), :]
            if u == 0:

                @pl.when(st == 1)
                def _():
                    pl.semaphore_wait(free.at[h], 1)

            zback(2 + st, h, s + 1, u).start()
            if u == SUBS - 1:

                @pl.when(st == 0)
                def _():
                    give_slot(h)

    def out_copy(st, h):
        return pltpu.make_async_copy(
            ag.at[st, h, pl.ds(0, tokens), :],
            (out_ref, dtok_ref)[st].at[:, pl.ds(h * hd, hd)],
            os_.at[st, h],
        )

    def finish(st):
        for h in range(2):
            for u in range(SUBS):
                zback(2 + st, h, NZ - 2, u).wait_recv()
            ag[st, h, 0:tokens, :] += land[h, NZ - 2]
            if st == 0:
                give_slot(h)
            out_copy(st, h).start()

    def weights(p):
        meta = meta_of(p)
        total = [jnp.zeros((1, 2 * tokens), F32)] * 4
        for blk in range(NX):
            at = pl.ds(blk * per, per)
            v = jnp.zeros((per, 1), F32)
            for h in range(2):
                v = v + jnp.sum(
                    q[0, h, p, at, :].astype(F32) * sx[1, h, p, at, :].astype(F32),
                    axis=1,
                    keepdims=True,
                )
            hit = row_masks(meta, x, z, cap, blk)
            c = row_weights(p, at)
            v = v / jnp.where(c > 0.0, c, 1.0)
            for k in range(4):
                total[k] = total[k] + jnp.sum(jnp.where(hit[k], v, 0.0), axis=0, keepdims=True)
        for i in range(2):
            for k in range(4):
                dacc[2 * p + i, k : k + 1, :] = total[k][:, i * tokens : (i + 1) * tokens]
            dacc[2 * p + i, 4:8, :] = jnp.zeros((4, tokens), F32)

    def nt_dot(a, b):
        return lax.dot_general(a, b, (((1,), (1,)), ((), ())), preferred_element_type=F32)

    def hidden_tile(f):
        at = rows_at(f, ft)
        dh = nt_dot(r[1, 0], wd[0, at, :]) + nt_dot(r[1, 1], wd[1, at, :])
        dga[f] = (dh * dga[f].astype(F32)).astype(BF)
        act[f] = (dh * act[f].astype(F32)).astype(BF)

    def row_tile(n):
        at = rows_at(n, dch)
        out = sum(
            nt_dot(dga[f], big[0, at, f * ft : (f + 1) * ft])
            + nt_dot(act[f], big[1, at, f * ft : (f + 1) * ft])
            for f in range(3)
        )
        each = chunks // 2
        sx[0, n // each, :, :, rows_at(n % each, dch)] = out.astype(BF).reshape(4, 4 * per, dch)

    def grad_chunk(c):
        each = chunks // 2
        lanes = rows_at(c % each, dch)
        a = r[0, c // each, :, lanes].T
        b = r[1, c // each, :, lanes].T
        for i, (lhs, rhs) in enumerate(((a, dga), (a, act), (b, hid))):
            for f in range(3):
                big[i, rows_at(c, dch), f * ft : (f + 1) * ft] = jnp.dot(
                    lhs, rhs[f], preferred_element_type=F32
                ).astype(BF)

    def grad_piece(k):
        mine = (k >= 4).astype(jnp.int32)
        kk = k - 4 * mine
        c = 2 * target(kk) + jnp.where(k >= 4, core, 1 - core)
        grad_chunk(c)

        @pl.when(k < 4)
        def _():
            ccopy(kk).start()

        @pl.when(k >= 4)
        def _():
            ccopy(kk).wait_recv()
            for i in range(3):
                big[i, rows_at(c, dch), :] += lc[kk, i]

            for i in range(2):

                @pl.when(kk == i)
                def _():
                    for g in range(3):
                        ycopy(i, 0, g).start()

    def dp_ring(n):
        s, g = n // 3, n % 3
        for i in range(2):
            b = (y + 2 * ny - 2 - s) % ny if i == 0 else (y + 2 + s) % ny
            ycopy(i, s, g).wait_recv()
            big[g, rows_at(2 * (2 * b + core) + i, half), :] += ly[i, s, g]

            @pl.when(s < ny - 2)
            def _():
                ycopy(i, s + 1, g).start()

    def piece(slot):
        @pl.when(slot == 10)
        def _():
            arrived(1)

        @pl.when((slot >= 10) & (slot < 16) & (slot % 2 == 0))
        def _():
            hidden_tile((slot - 10) // 2)

        @pl.when((slot >= 15) & (slot < 15 + chunks))
        def _():
            row_tile(slot - 15)

        @pl.when((slot >= 23) & (slot < 31))
        def _():
            grad_piece(slot - 23)

        @pl.when((slot >= 33) & (slot < 60) & (slot % 3 == 0))
        def _():
            dp_ring((slot - 33) // 3)

    @pl.loop(0, 16)
    def _(t):
        st, j, h, p = where_at(t)

        @pl.when(t + 3 < 16)
        def _():
            send(t + 3)

        @pl.when(t == 7)
        def _():
            sent_out(1)

        scatter(t)

        @pl.when(j < 2)
        def _():
            for hh in range(2):

                @pl.when(h == hh)
                def _():
                    @pl.when(st == 1)
                    def _():
                        pl.semaphore_wait(free.at[hh], 1)

                    for u in range(SUBS):
                        zback(2 + st, hh, 0, u).start()

        for u in range(SUBS):

            @pl.when(j >= 2)
            def _():
                ring_back(st, j - 2, u)

            piece(SUBS * t + u)
            if u == 1:

                @pl.when(t + 2 < 16)
                def _():
                    forward_back(t + 2)

        @pl.when(t == 9)
        def _():
            finish(0)

        @pl.when((t == 9) | (t == 10) | (t == 12) | (t == 14))
        def _():
            weights((t - 8) // 2)

        @pl.when(t == 9)
        def _():
            dcopy(0).start()

        @pl.when(t >= 10)
        def _():
            s = t - 10
            dcopy(s).wait_recv()
            dacc[s + 2] += dland[s]
            dcopy(s + 1).start()

    wd[0, :, 0:dch] = big[2, rows_at(dp, dch), :].T
    last = [
        pltpu.make_async_copy(big.at[0, rows_at(dp, dch), :], dwg_ref, os_.at[2, 0]),
        pltpu.make_async_copy(big.at[1, rows_at(dp, dch), :], dwu_ref, os_.at[2, 1]),
        pltpu.make_async_copy(wd.at[0, :, pl.ds(0, dch)], dwd_ref, os_.at[3, 0]),
    ]
    for c in last:
        c.start()
    finish(1)
    dcopy(NZ - 2).wait_recv()
    dcomb_ref[...] = dacc[0] + dland[NZ - 2]

    xsent_out(1)
    for h, n in ((0, 4), (1, 3)):
        for s in range(n):
            mcopy(h, s).wait_send()

    @pl.loop(2, 4)
    def _(st):
        for h in range(2):

            @pl.loop(0, NZ - 1)
            def _(s):
                for u in range(SUBS):
                    zback(st, h, s, u).wait_send()

        @pl.loop(0, 8)
        def _(i):
            for k in range(3):
                xback(st, i // 4, i % 4, k, prod).wait_send()
            fback(st, i // 4, i % 4).wait_send()

    @pl.loop(0, NZ - 1)
    def _(s):
        dcopy(s).wait_send()

    @pl.loop(0, 4)
    def _(k):
        ccopy(k).wait_send()

    @pl.loop(0, 9)
    def _(n):
        for i in range(2):
            ycopy(i, n // 3, n % 3).wait_send()

    for c in last:
        c.wait()
    for st in range(2):
        for h in range(2):
            out_copy(st, h).wait()


def layer(tokens, cotangent, routes, combine, w_gate, w_up, w_down, cap):
    n, features = tokens.shape
    ff = w_gate.shape[1]
    hd = features // 2
    per = 2 * cap
    rows = 16 * per
    ft = ff // 3
    ndp = lax.axis_size("dp")
    dch = features // ndp
    ny = ndp // 2
    dma = pltpu.SemaphoreType.DMA
    vmem = pl.BlockSpec(memory_space=pltpu.VMEM)
    hbm = pl.BlockSpec(memory_space=pl.ANY)
    share = jax.ShapeDtypeStruct((dch, ff), BF)
    full = jax.ShapeDtypeStruct((n, features), BF)
    return pl.pallas_call(
        functools.partial(layer_kernel, cap),
        out_shape=(
            full,
            full,
            jax.ShapeDtypeStruct((8, n), F32),
            share,
            share,
            jax.ShapeDtypeStruct((ff, dch), BF),
        ),
        in_specs=[hbm, hbm, vmem, vmem, hbm, hbm, hbm],
        out_specs=(hbm, hbm, vmem, hbm, hbm, hbm),
        scratch_shapes=[
            pltpu.VMEM((2, 2, NZ * n, hd), BF),
            pltpu.VMEM((2, 2, 4, 4 * per, hd), BF),
            pltpu.VMEM((2, 2, rows, hd), BF),
            pltpu.VMEM((4, 2, 4, per, hd), BF),
            pltpu.VMEM((2, 2, 4, 4 * per, hd), BF),
            pltpu.VMEM((2, NZ - 1, n, hd), BF),
            pltpu.VMEM((3, features, ff), BF),
            pltpu.VMEM((2, ff, hd), BF),
            pltpu.VMEM((rows, ft), F32),
            pltpu.VMEM((3, rows, ft), BF),
            pltpu.VMEM((3, rows, ft), BF),
            pltpu.VMEM((3, rows, ft), BF),
            pltpu.VMEM((2, 4, 4 * per, hd), BF),
            pltpu.VMEM((4, 3, dch, ff), BF),
            pltpu.VMEM((2, ny - 1, 3, dch // 2, ff), BF),
            pltpu.VMEM((NZ, 8, n), F32),
            pltpu.VMEM((4, 4 * per, 2 * n), BF),
            pltpu.VMEM((4 * per, 128), F32),
            pltpu.VMEM((4 * per, 2 * n), F32),
            pltpu.VMEM((2, 4, 2 * n, 4 * per), BF),
            pltpu.VMEM((NZ, 8, n), F32),
            pltpu.VMEM((NZ - 1, 8, n), F32),
            dma((4, 2, NZ - 1, SUBS)),
            dma((4, 2, NZ - 1, SUBS)),
            dma((2, 4)),
            dma((2, 4)),
            dma((4, 2, 4, 3)),
            dma((4, 2, 4, 3)),
            dma((4, 2, 4)),
            dma((4, 2, 4)),
            dma((2, 2, 4)),
            dma((8,)),
            dma((4, 2)),
            dma((NZ - 1,)),
            dma((NZ - 1,)),
            dma((4,)),
            dma((4,)),
            dma((2, ny - 1, 3)),
            dma((2, ny - 1, 3)),
            pltpu.SemaphoreType.REGULAR((2,)),
        ],
        compiler_params=pltpu.CompilerParams(
            collective_id=0, has_side_effects=True, vmem_limit_bytes=67043328
        ),
        name="layer",
    )(tokens, cotangent, routes, combine, w_gate, w_up, w_down)


def close_kernel(*refs):
    n = len(refs) // 2
    for src, dst in zip(refs[:n], refs[n:]):
        dst[...] = src[: dst.shape[0]]


def close(arrays, top):
    vmem = pl.BlockSpec(memory_space=pltpu.VMEM)
    shapes = [jax.ShapeDtypeStruct(a.shape, a.dtype) for a in arrays]
    shapes[2] = jax.ShapeDtypeStruct((top, arrays[2].shape[1]), F32)
    return pl.pallas_call(
        close_kernel,
        out_shape=tuple(shapes),
        in_specs=[vmem] * len(arrays),
        out_specs=(vmem,) * len(arrays),
        name="close",
    )(*arrays)


def per_device(tokens, routes, combine, cotangent, w_gate, w_up, w_down):
    n = tokens.shape[0]
    per_token = routes.shape[1]
    experts = w_gate.shape[0] * lax.axis_size("expert")
    cap = 3 * n * per_token // (2 * experts)
    arrays = layer(
        tokens, cotangent, routes.T, combine.T, w_gate[0], w_up[0], w_down[0], cap
    )
    output, d_tokens, d_comb, d_w_gate, d_w_up, d_w_down = close(arrays, per_token)
    return output, d_tokens, d_comb.T, d_w_gate[None], d_w_up[None], d_w_down[None]


def solution(mesh):
    row = P(("dp", "expert"), None)
    weight = P("expert", None, None)
    return jax.shard_map(
        per_device,
        mesh=mesh,
        in_specs=(row, row, row, row, weight, weight, weight),
        out_specs=(
            row,
            row,
            row,
            P("expert", "dp", None),
            P("expert", "dp", None),
            P("expert", None, "dp"),
        ),
        check_vma=False,
    )
```

time: 435 us -> 217 us (0.50); the launches traced: 427 us -> 217 us
  Pallas kernels: 0 us -> 217 us
  waiting for transfers between devices: 174 us -> 0 us
  blocking collectives: 84.8 us -> 0 us
  local copies, waits for them, and re-layouts: 53.4 us -> 0 us
  matrix products: 49.3 us -> 0 us
  starting transfers between devices: 27.1 us -> 0 us
  other arithmetic: 24.7 us -> 0 us
  between operations: 14.3 us -> 0.64 us
    pallas_call x0 -> x2, Pallas kernels: none -> 217 us  [the longest x1 214 us: layer(): pl.pallas_call(functools.partial(layer_kernel, cap), out_shape=(full, ful...]
    all_to_all x3 -> x0, waiting for transfers between devices: 174 us -> none  [the longest x1 60.4 us: per_device(): lax.all_to_all(d_rows, 'expert', split_axis=0, concat_axis=0, tiled=True)]
    all_to_all x1 -> x0, blocking collectives: 84.8 us -> none  [per_device(): lax.all_to_all(outgoing, 'expert', split_axis=0, concat_axis=0, tiled=True)]
    dot_general x9 -> x0, matrix products: 49.3 us -> none  [the longest x1 6.88 us: per_device(): jnp.einsum('secd,edf->secf', arrived, w_up, preferred_element_type=jnp.fl...]
    gather x4 -> x0, local copies, waits for them, and re-layouts: 28.2 us -> none  [the longest x1 8.96 us: per_device(): scaled[pair_index]]
    all_to_all x3 -> x0, starting transfers between devices: 15.2 us -> none  [the longest x1 5.19 us: per_device(): lax.all_to_all(outgoing_grad, 'expert', split_axis=0, concat_axis=0, tile...]
    reduce_scatter x3 -> x0, starting transfers between devices: 11.9 us -> none  [the longest x1 11.6 us: per_device(): lax.psum_scatter(part_gate.astype(jnp.bfloat16), 'dp', scatter_dimension=...]
    reduce_sum x3 -> x0, other arithmetic: 11.7 us -> none  [the longest x1 6.63 us: per_device(): d_combine = jnp.sum(per_slot * cot_float[:, None, :], axis=2)]
  transfers between devices with their start and end apart: 6 -> 0, of which waited for: 3 -> 0; matrix products, arithmetic and copies ran while one was open for 16% -> 0% of each run, Pallas kernels for 0% -> 0%
where the time goes in v4:
time: 217 us
  Pallas kernels  217 us (100%)
    pallas_call x1, Pallas kernels, layer(): pl.pallas_call(functools.partial(layer_kernel, cap), out_shape=(full, ful...  214 us

profile of v4, /device:TPU:8, one launch (start us, length us, event | category | flops | bytes accessed | tf_op | source)
XLA Modules:
  0.0 217.1 jit_solution(15925458499576570153)
XLA Ops:
  0.6 213.6 %layer.1 = (bf16[128,2048]{1,0:T(8,128)(2,1)}, bf16[128,2048]{1,0:T(8,128)(2,1)}, f32[8,128]{1,0:T(8,128)}, bf16[256,768]{1,0:T(8,128)(2,1)}, bf16[256,768]{1,0:T(8,128)(2,1)}, /*index=5*/bf16[768,256]{1,0:T(8,128)(2,1)}) custom-call(bf16[128,2048]{1,0:T(8,128)(2,1)} %tok_ref.1, bf16[128,2048]{1,0:T(8,128)(2,1)} %cot_ref.1, s32[4,128]{1,0:T(4,128)} %bitcast.12, ...), custom_call_target="tpu_custom_call" | custom-call | tf_op jit(solution)/shard_map/layer/pallas_call | solution.py:750
  214.2 2.9 %close.1 = (bf16[128,2048]{1,0:T(8,128)(2,1)}, bf16[128,2048]{1,0:T(8,128)(2,1)}, f32[4,128]{1,0:T(4,128)}, bf16[256,768]{1,0:T(8,128)(2,1)}, bf16[256,768]{1,0:T(8,128)(2,1)}, /*index=5*/bf16[768,256]{1,0:T(8,128)(2,1)}) custom-call(bf16[128,2048]{1,0:T(8,128)(2,1)} %get-tuple-element.18.refs_0_, bf16[128,2048]{1,0:T(8,128)(2,1)} %get-tuple-element.19.refs_1_, ...), custom_call_target="tpu_custom_call" | custom-call | tf_op jit(solution)/shard_map/close/pallas_call | solution.py:821

commit v5 on v4

--- a/solution.py
+++ b/solution.py
@@ -10,6 +10,11 @@
 MESH = pl.DeviceIdType.MESH
 NZ = 8
 NX = 4
+FOUT = 0
+LATE = 2
+PAIR = 30
+RING = 36
+AHEAD = 3
 SUBS = 4
 BF = jnp.bfloat16
 F32 = jnp.float32
@@ -378,9 +383,11 @@
     def _(t):
         st, j, h, p = where_at(t)
 
-        @pl.when(t == 14)
-        def _():
-            send(0)
+        for i in range(2):
+
+            @pl.when(t == 13 + i)
+            def _():
+                send(i)
 
         @pl.when(st == 0)
         def _():
@@ -404,25 +411,33 @@
                     for i in range(4, 8):
                         load(i).wait()
 
-                @pl.when((t >= 10) & (t < 13))
-                def _():
-                    gate_tile(t - 10)
+            slot = SUBS * (t - 10) + u
+
+            @pl.when((slot >= 0) & (slot < 6))
+            def _():
+                if u % 2 == 0:
+                    gate_tile(slot // 2)
+                else:
+                    up_tile(slot // 2)
+
+            for i in range(4):
+                if (6 + i) % SUBS == u:
+
+                    @pl.when(slot == 6 + i)
+                    def _():
+                        down_tile(i)
+
+            if u == FOUT:
+
+                @pl.when(t >= LATE)
+                def _():
+                    forward_out(t - LATE)
 
             if u == 1:
 
-                @pl.when(t > 0)
-                def _():
-                    forward_out(t - 1)
-
-            if u == 2:
-
-                @pl.when((t >= 10) & (t < 13))
-                def _():
-                    up_tile(t - 10)
-
-            @pl.when(t == 13)
-            def _():
-                down_tile(u)
+                @pl.when(t == 15)
+                def _():
+                    forward_back(0)
 
         @pl.when(t < 4)
         def _():
@@ -437,13 +452,10 @@
         for i in range(3):
             xout(st, h, p, i).start()
 
-        @pl.when(t == 15)
-        def _():
-            send(1)
-
-    forward_out(15)
-    forward_back(0)
-    send(2)
+    for i in range(LATE):
+        forward_out(16 - LATE + i)
+    for i in range(2, AHEAD):
+        send(i)
 
     def sent_out(st):
         for h in range(2):
@@ -462,7 +474,8 @@
 
     sent_out(0)
     xsent_out(0)
-    forward_back(1)
+    for i in range(1, AHEAD - 1):
+        forward_back(i)
 
     def scatter(t):
         st, _, h, p = where_at(t)
@@ -539,9 +552,11 @@
     def nt_dot(a, b):
         return lax.dot_general(a, b, (((1,), (1,)), ((), ())), preferred_element_type=F32)
 
-    def hidden_tile(f):
-        at = rows_at(f, ft)
-        dh = nt_dot(r[1, 0], wd[0, at, :]) + nt_dot(r[1, 1], wd[1, at, :])
+    def hidden_first(f):
+        gate[...] = nt_dot(r[1, 0], wd[0, rows_at(f, ft), :])
+
+    def hidden_second(f):
+        dh = gate[...] + nt_dot(r[1, 1], wd[1, rows_at(f, ft), :])
         dga[f] = (dh * dga[f].astype(F32)).astype(BF)
         act[f] = (dh * act[f].astype(F32)).astype(BF)
 
@@ -567,27 +582,25 @@
                 ).astype(BF)
 
     def grad_piece(k):
-        mine = (k >= 4).astype(jnp.int32)
-        kk = k - 4 * mine
-        c = 2 * target(kk) + jnp.where(k >= 4, core, 1 - core)
-        grad_chunk(c)
+        kk = k % 4
+        grad_chunk(2 * target(kk) + jnp.where(k >= 4, core, 1 - core))
 
         @pl.when(k < 4)
         def _():
             ccopy(kk).start()
 
-        @pl.when(k >= 4)
-        def _():
-            ccopy(kk).wait_recv()
-            for i in range(3):
-                big[i, rows_at(c, dch), :] += lc[kk, i]
-
-            for i in range(2):
-
-                @pl.when(kk == i)
-                def _():
-                    for g in range(3):
-                        ycopy(i, 0, g).start()
+    def pair_sum(k):
+        at = rows_at(2 * target(k) + core, dch)
+        ccopy(k).wait_recv()
+        for i in range(3):
+            big[i, at, :] += lc[k, i]
+
+        for i in range(2):
+
+            @pl.when(k == i)
+            def _():
+                for g in range(3):
+                    ycopy(i, 0, g).start()
 
     def dp_ring(n):
         s, g = n // 3, n % 3
@@ -605,29 +618,39 @@
         def _():
             arrived(1)
 
-        @pl.when((slot >= 10) & (slot < 16) & (slot % 2 == 0))
-        def _():
-            hidden_tile((slot - 10) // 2)
-
-        @pl.when((slot >= 15) & (slot < 15 + chunks))
-        def _():
-            row_tile(slot - 15)
-
-        @pl.when((slot >= 23) & (slot < 31))
-        def _():
-            grad_piece(slot - 23)
-
-        @pl.when((slot >= 33) & (slot < 60) & (slot % 3 == 0))
-        def _():
-            dp_ring((slot - 33) // 3)
+        @pl.when((slot >= 10) & (slot < 16))
+        def _():
+            @pl.when(slot % 2 == 0)
+            def _():
+                hidden_first((slot - 10) // 2)
+
+            @pl.when(slot % 2 == 1)
+            def _():
+                hidden_second((slot - 10) // 2)
+
+        @pl.when((slot >= 16) & (slot < 16 + chunks))
+        def _():
+            row_tile(slot - 16)
+
+        @pl.when((slot >= 24) & (slot < 32))
+        def _():
+            grad_piece(slot - 24)
+
+        @pl.when((slot >= PAIR) & (slot < PAIR + 4))
+        def _():
+            pair_sum(slot - PAIR)
+
+        @pl.when((slot >= RING) & (slot < RING + 27) & ((slot - RING) % 3 == 0))
+        def _():
+            dp_ring((slot - RING) // 3)
 
     @pl.loop(0, 16)
     def _(t):
         st, j, h, p = where_at(t)
 
-        @pl.when(t + 3 < 16)
-        def _():
-            send(t + 3)
+        @pl.when(t + AHEAD < 16)
+        def _():
+            send(t + AHEAD)
 
         @pl.when(t == 7)
         def _():
@@ -657,9 +680,9 @@
             piece(SUBS * t + u)
             if u == 1:
 
-                @pl.when(t + 2 < 16)
-                def _():
-                    forward_back(t + 2)
+                @pl.when(t + AHEAD - 1 < 16)
+                def _():
+                    forward_back(t + AHEAD - 1)
 
         @pl.when(t == 9)
         def _():

time: 217 us -> 209 us (0.963)
  Pallas kernels: 217 us -> 208 us
    pallas_call x1, Pallas kernels: 214 us -> 205 us  [layer(): pl.pallas_call(functools.partial(layer_kernel, cap), out_shape=(full, ful...]
where the time goes in v5:
time: 209 us
  Pallas kernels  208 us (100%)
    pallas_call x1, Pallas kernels, layer(): pl.pallas_call(functools.partial(layer_kernel, cap), out_shape=(full, ful...  205 us

profile of v5, /device:TPU:8, one launch (start us, length us, event | category | flops | bytes accessed | tf_op | source)
XLA Modules:
  0.0 208.7 jit_solution(7751199327775923441)
XLA Ops:
  0.6 205.1 %layer.1 = (bf16[128,2048]{1,0:T(8,128)(2,1)}, bf16[128,2048]{1,0:T(8,128)(2,1)}, f32[8,128]{1,0:T(8,128)}, bf16[256,768]{1,0:T(8,128)(2,1)}, bf16[256,768]{1,0:T(8,128)(2,1)}, /*index=5*/bf16[768,256]{1,0:T(8,128)(2,1)}) custom-call(bf16[128,2048]{1,0:T(8,128)(2,1)} %tok_ref.1, bf16[128,2048]{1,0:T(8,128)(2,1)} %cot_ref.1, s32[4,128]{1,0:T(4,128)} %bitcast.12, ...), custom_call_target="tpu_custom_call" | custom-call | tf_op jit(solution)/shard_map/layer/pallas_call | solution.py:773
  205.7 2.9 %close.1 = (bf16[128,2048]{1,0:T(8,128)(2,1)}, bf16[128,2048]{1,0:T(8,128)(2,1)}, f32[4,128]{1,0:T(4,128)}, bf16[256,768]{1,0:T(8,128)(2,1)}, bf16[256,768]{1,0:T(8,128)(2,1)}, /*index=5*/bf16[768,256]{1,0:T(8,128)(2,1)}) custom-call(bf16[128,2048]{1,0:T(8,128)(2,1)} %get-tuple-element.18.refs_0_, bf16[128,2048]{1,0:T(8,128)(2,1)} %get-tuple-element.19.refs_1_, ...), custom_call_target="tpu_custom_call" | custom-call | tf_op jit(solution)/shard_map/close/pallas_call | solution.py:844

commit v6 on v5

--- a/solution.py
+++ b/solution.py
@@ -12,8 +12,8 @@
 NX = 4
 FOUT = 0
 LATE = 2
-PAIR = 30
-RING = 36
+PAIR = 32
+RING = 37
 AHEAD = 3
 SUBS = 4
 BF = jnp.bfloat16
@@ -383,12 +383,6 @@
     def _(t):
         st, j, h, p = where_at(t)
 
-        for i in range(2):
-
-            @pl.when(t == 13 + i)
-            def _():
-                send(i)
-
         @pl.when(st == 0)
         def _():
             for hh, n in ((0, 4), (1, 3)):
@@ -433,11 +427,19 @@
                 def _():
                     forward_out(t - LATE)
 
-            if u == 1:
-
-                @pl.when(t == 15)
-                def _():
-                    forward_back(0)
+            if u == 2:
+                for i in range(3):
+
+                    @pl.when(t == 12 + i)
+                    def _():
+                        send(i)
+
+            if u == 3:
+                for i in range(2):
+
+                    @pl.when(t == 14 + i)
+                    def _():
+                        forward_back(i)
 
         @pl.when(t < 4)
         def _():
@@ -452,10 +454,7 @@
         for i in range(3):
             xout(st, h, p, i).start()
 
-    for i in range(LATE):
-        forward_out(16 - LATE + i)
-    for i in range(2, AHEAD):
-        send(i)
+    forward_out(14)
 
     def sent_out(st):
         for h in range(2):
@@ -473,9 +472,6 @@
             fout(st, i // 4, i % 4).wait_send()
 
     sent_out(0)
-    xsent_out(0)
-    for i in range(1, AHEAD - 1):
-        forward_back(i)
 
     def scatter(t):
         st, _, h, p = where_at(t)
@@ -678,11 +674,22 @@
                 ring_back(st, j - 2, u)
 
             piece(SUBS * t + u)
+            if u == 0:
+
+                @pl.when(t == 0)
+                def _():
+                    forward_back(2)
+
             if u == 1:
 
-                @pl.when(t + AHEAD - 1 < 16)
-                def _():
-                    forward_back(t + AHEAD - 1)
+                @pl.when(t == 0)
+                def _():
+                    forward_out(15)
+                    xsent_out(0)
+
+                @pl.when((t >= 1) & (t + 2 < 16))
+                def _():
+                    forward_back(t + 2)
 
         @pl.when(t == 9)
         def _():

time: 209 us -> 206 us (0.986)
  Pallas kernels: 208 us -> 205 us
    pallas_call x1, Pallas kernels: 205 us -> 202 us  [layer(): pl.pallas_call(functools.partial(layer_kernel, cap), out_shape=(full, ful...]
where the time goes in v6:
time: 206 us
  Pallas kernels  205 us (100%)
    pallas_call x1, Pallas kernels, layer(): pl.pallas_call(functools.partial(layer_kernel, cap), out_shape=(full, ful...  202 us

profile of v6, /device:TPU:8, one launch (start us, length us, event | category | flops | bytes accessed | tf_op | source)
XLA Modules:
  0.0 205.9 jit_solution(17031818340985579162)
XLA Ops:
  0.6 202.4 %layer.1 = (bf16[128,2048]{1,0:T(8,128)(2,1)}, bf16[128,2048]{1,0:T(8,128)(2,1)}, f32[8,128]{1,0:T(8,128)}, bf16[256,768]{1,0:T(8,128)(2,1)}, bf16[256,768]{1,0:T(8,128)(2,1)}, /*index=5*/bf16[768,256]{1,0:T(8,128)(2,1)}) custom-call(bf16[128,2048]{1,0:T(8,128)(2,1)} %tok_ref.1, bf16[128,2048]{1,0:T(8,128)(2,1)} %cot_ref.1, s32[4,128]{1,0:T(4,128)} %bitcast.12, ...), custom_call_target="tpu_custom_call" | custom-call | tf_op jit(solution)/shard_map/layer/pallas_call | solution.py:780
  203.0 2.9 %close.1 = (bf16[128,2048]{1,0:T(8,128)(2,1)}, bf16[128,2048]{1,0:T(8,128)(2,1)}, f32[4,128]{1,0:T(4,128)}, bf16[256,768]{1,0:T(8,128)(2,1)}, bf16[256,768]{1,0:T(8,128)(2,1)}, /*index=5*/bf16[768,256]{1,0:T(8,128)(2,1)}) custom-call(bf16[128,2048]{1,0:T(8,128)(2,1)} %get-tuple-element.18.refs_0_, bf16[128,2048]{1,0:T(8,128)(2,1)} %get-tuple-element.19.refs_1_, ...), custom_call_target="tpu_custom_call" | custom-call | tf_op jit(solution)/shard_map/close/pallas_call | solution.py:851
